TPU v7x, 32 devices: a whole 2x2x4 slice. The times are simulated.
32 devices in a mesh: groups: 2 (over y), ctx: 4 (over z), head: 2 (over x), sub: 2 (over core).
Axes of the slice: x: 2, y: 2, z: 4, core: 2. Of those that a mesh axis runs over, the one named last changes fastest.
Arguments:
- tokens: bfloat16 [16384, 3584], P(('groups', 'ctx', 'sub'), 'head'), parts along dimension 0, may hold values from -40 to 40
- q_weight: bfloat16 [3584, 3584], P('sub', 'head'), may hold values from -0.09375 to 0.09375
- k_weight: bfloat16 [3584, 512], P('sub', 'head'), may hold values from -0.09375 to 0.09375
- v_weight: bfloat16 [3584, 512], P('sub', 'head'), may hold values from -0.09375 to 0.09375
- q_bias: float32 [3584], P('head'), may hold values from -3 to 3
- v_bias: float32 [512], P('head'), may hold values from -3 to 3
Outputs:
- head_outputs: bfloat16 [16384, 3584], P(('groups', 'ctx', 'sub')), parts along dimension 0
There are 2 independent parts, one for each index of `groups`. A program takes and returns all parts, laid end to end along the dimension named above; an argument that names none is the same for every part. Nothing has to cross between parts.
All inputs are finite; a program needn't handle non-finite values.
Results may differ from a plain program's by a relative error of at most 0.0059.
Values may be sent and summed in bfloat16 or wider, within the bound.
No kernel may reach another device: no remote copies, remote signals or barrier semaphores. Data moves between devices by JAX's collectives and lax.ppermute only.
A program may use at most 128 MiB of HBM per device.

v0:
```python
import functools
import math

import jax
import jax.numpy as jnp
from jax import lax
from jax.experimental import pallas as pl
from jax.experimental.pallas import tpu as pltpu
from jax.sharding import PartitionSpec as P


HQ = 28
KVH = 4
HD = 128
BLOCK = 128
NEAR = (0, 1, 2, 4)
GROUP = HQ // KVH


def shifted(value, axis, steps):
    count = lax.axis_size(axis)
    return lax.ppermute(value, axis, [(s, (s + steps) % count) for s in range(count)])


def swapped(value, axis):
    return lax.ppermute(value, axis, [(0, 1), (1, 0)])


def rotary_tables(positions):
    half = HD // 2
    freqs = jnp.exp(-(2.0 * jnp.arange(half, dtype=jnp.float32) / (2 * half)) * math.log(1000000.0))
    angle = positions[:, None] * freqs[None, :]
    cosine = jnp.cos(angle)
    sine = jnp.sin(angle)
    return jnp.concatenate([cosine, cosine], 1), jnp.concatenate([-sine, sine], 1)


VMEM = pl.BlockSpec(memory_space=pltpu.VMEM)
SMEM = pl.BlockSpec(memory_space=pltpu.SMEM)
ANY = pl.BlockSpec(memory_space=pl.ANY)
HBM = pl.BlockSpec(memory_space=pltpu.HBM)


def params(mib):
    return pltpu.CompilerParams(vmem_limit_bytes=mib * 2**20)


def stage_body(n, flag, *refs):
    own, other, outs, sems = refs[:n], refs[n : 2 * n], refs[2 * n : -1], refs[-1]

    def bring(first, second):
        copies = []
        for half, sources in enumerate((first, second)):
            q_out, kv_out = outs[2 * half], outs[2 * half + 1]
            nk = sources[1].shape[1]
            targets = (q_out, kv_out.at[:, pl.ds(0, nk)], kv_out.at[:, pl.ds(nk, nk)])
            for i, (source, target) in enumerate(zip(sources, targets)):
                copies.append(pltpu.make_async_copy(source, target, sems.at[half, i]))
        for copy in copies:
            copy.start()
        for copy in copies:
            copy.wait()

    @pl.when(flag[0] == 1)
    def _():
        bring(own, other)

    @pl.when(flag[0] != 1)
    def _():
        bring(other, own)


def stage(flag, own, other):
    half, nq = own[0].shape
    nk = own[1].shape[1]
    shapes = [pltpu.VMEM((half, nq), jnp.bfloat16), pltpu.VMEM((half, 2 * nk), jnp.bfloat16)] * 2
    return pl.pallas_call(
        functools.partial(stage_body, len(own)),
        out_shape=tuple(shapes),
        in_specs=[SMEM] + [HBM] * (2 * len(own)),
        out_specs=(VMEM,) * 4,
        scratch_shapes=[pltpu.SemaphoreType.DMA((2, len(own)))],
        compiler_params=params(2),
        cost_estimate=pl.CostEstimate(flops=0, bytes_accessed=4 * half * (nq + 2 * nk), transcendentals=0),
        name="stage",
    )(flag, *own, *other)


def project_body(row, tile, rot, ta, tb, wa, wb, bias, cos, sin, *refs):
    out = refs[-1]
    rows = tb.shape[0]
    mine = pl.ds(row, rows)

    def columns(i):
        at = pl.ds(pl.multiple_of(i * tile, tile), tile)
        acc = jnp.dot(ta[mine, :], wa[:, at], preferred_element_type=jnp.float32)
        acc = acc + jnp.dot(tb[...], wb[:, at], preferred_element_type=jnp.float32)
        acc = acc + bias[:, at]
        heads = []
        for h in range(tile // HD):
            v = acc[:, h * HD : (h + 1) * HD]
            if h < rot:
                v = v * cos[mine, :] + pltpu.roll(v, HD // 2, 1) * sin[mine, :]
            heads.append(v.astype(jnp.bfloat16))
        out[:, at] = jnp.concatenate(heads, 1)

    if tile == out.shape[1]:
        columns(0)
    else:
        pl.loop(0, out.shape[1] // tile)(columns)


def project(tokens, row, piece, wa, wb, bias, cos, sin, tile, rot, deps):
    rows, half = piece.shape
    cols = wa.shape[1]
    return pl.pallas_call(
        functools.partial(project_body, row, tile, rot),
        out_shape=jax.ShapeDtypeStruct((rows, cols), jnp.bfloat16),
        in_specs=[VMEM] * 7 + [ANY] * len(deps),
        out_specs=VMEM,
        compiler_params=params(8),
        cost_estimate=pl.CostEstimate(flops=4 * rows * half * cols, bytes_accessed=0, transcendentals=0),
    )(tokens, piece, wa, wb, bias, cos, sin, *deps)


def attend_body(plan, n_arrays, kvl, bias, *refs):
    nb = len(plan)
    arrays = refs[nb : nb + n_arrays]
    out = refs[-1]
    scale = math.log2(math.e) / math.sqrt(HD)
    lower = lax.broadcasted_iota(jnp.int32, (BLOCK, BLOCK), 0) >= lax.broadcasted_iota(
        jnp.int32, (BLOCK, BLOCK), 1
    )

    def kv_head(g):
        for j, (q_row, slots) in enumerate(plan):
            n = len(slots)
            k_at = pl.ds(pl.multiple_of(g * HD, HD), HD)
            v_at = pl.ds(pl.multiple_of((kvl + g) * HD, HD), HD)
            keys = jnp.concatenate([arrays[a][r * BLOCK : (r + 1) * BLOCK, k_at] for a, r in slots], 0)
            vals = jnp.concatenate([arrays[a][r * BLOCK : (r + 1) * BLOCK, v_at] for a, r in slots], 0)
            vals = jnp.concatenate([vals, jnp.ones_like(vals)], 1)
            for h in range(GROUP):
                at = pl.ds(pl.multiple_of((g * GROUP + h) * HD, HD), HD)
                s = lax.dot_general(
                    refs[j][q_row * BLOCK : (q_row + 1) * BLOCK, at], keys, (((1,), (1,)), ((), ())),
                    preferred_element_type=jnp.float32,
                )
                parts = [jnp.where(lower, s[:, :BLOCK], -1e30)]
                for t in range(1, n):
                    parts.append(s[:, t * BLOCK : (t + 1) * BLOCK] + bias[j * n + t])
                s = jnp.concatenate(parts, 1)
                peak = jnp.max(s, axis=1, keepdims=True)
                p = jnp.exp2((s - peak) * scale).astype(jnp.bfloat16)
                o = jnp.dot(p, vals, preferred_element_type=jnp.float32)
                out[j * BLOCK : (j + 1) * BLOCK, at] = (o[:, :HD] / o[:, HD:]).astype(jnp.bfloat16)

    if kvl == 1:
        kv_head(0)
    else:
        pl.loop(0, kvl)(kv_head)


def attend(bias, queries, arrays, plan, kvl, deps):
    nb = len(queries)
    width = kvl * GROUP * HD
    keys = len(plan[0]) * BLOCK
    plan = [(r, slots) for (_, r), slots in zip(queries, plan)]
    return pl.pallas_call(
        functools.partial(attend_body, plan, len(arrays), kvl),
        out_shape=jax.ShapeDtypeStruct((nb * BLOCK, width), jnp.bfloat16),
        in_specs=[SMEM] + [VMEM] * (nb + len(arrays)) + [ANY] * len(deps),
        out_specs=VMEM,
        compiler_params=params(8),
        cost_estimate=pl.CostEstimate(
            flops=8 * nb * width * keys * BLOCK,
            bytes_accessed=0,
            transcendentals=nb * BLOCK * kvl * GROUP * keys,
        ),
        name="attend",
    )(bias, *[a for a, _ in queries], *arrays, *deps)


def cut_body(row, source, out, sem):
    copy = pltpu.make_async_copy(source.at[pl.ds(row, out.shape[0]), :], out, sem)
    copy.start()
    copy.wait()


def cut(source, block, count):
    return pl.pallas_call(
        functools.partial(cut_body, block * BLOCK),
        out_shape=pltpu.VMEM((count * BLOCK, source.shape[1]), source.dtype),
        in_specs=[HBM],
        out_specs=VMEM,
        scratch_shapes=[pltpu.SemaphoreType.DMA],
        compiler_params=params(2),
        cost_estimate=pl.CostEstimate(
            flops=0, bytes_accessed=2 * count * BLOCK * source.shape[1], transcendentals=0
        ),
        name="cut",
    )(source)


def place_body(side, src, *rest):
    rest[-1][...] = src[...]


def place(total, piece, side, blocks, shape):
    nb = len(blocks)
    cols = piece.shape[1]
    step = blocks[1] - blocks[0] if nb > 1 else 0
    in_specs = [pl.BlockSpec((BLOCK, cols), lambda i, s: (i, 0))]
    args = [piece]
    aliases = {}
    if total is not None:
        in_specs.append(pl.BlockSpec(memory_space=pl.ANY))
        args.append(total)
        aliases = {2: 0}
    return pl.pallas_call(
        place_body,
        out_shape=jax.ShapeDtypeStruct(shape, jnp.bfloat16),
        grid_spec=pltpu.PrefetchScalarGridSpec(
            num_scalar_prefetch=1,
            grid=(nb,),
            in_specs=in_specs,
            out_specs=pl.BlockSpec((BLOCK, cols), lambda i, s: (blocks[0] + i * step, s[0])),
        ),
        input_output_aliases=aliases,
        compiler_params=params(4),
        cost_estimate=pl.CostEstimate(flops=0, bytes_accessed=4 * nb * BLOCK * cols, transcendentals=0),
        name="place",
    )(side, *args)


def chunks_of(blocks):
    n = blocks // 4
    return [(quarter * n, n) for quarter in (2, 0, 1, 3)]


def layer(tokens, q_weight, k_weight, v_weight, q_bias, v_bias):
    n_sub = lax.axis_size("sub")
    n_ctx = lax.axis_size("ctx")
    n_head = lax.axis_size("head")
    rows = tokens.shape[0]
    blocks = rows // BLOCK
    kvl = k_weight.shape[1] // HD
    sub = lax.axis_index("sub")
    ctx = lax.axis_index("ctx")
    head = lax.axis_index("head")
    shard = ctx * n_sub + sub
    runs = chunks_of(blocks)

    paired = n_head == 2
    if paired:
        pieces = []
        for b, n in runs:
            pieces.append(swapped(cut(tokens, b, n), "head"))
        flag = (sub == head).astype(jnp.int32).reshape(1)
    else:
        features = lax.all_gather(tokens, "head", axis=1, tiled=True)
        half = features.shape[1] // n_sub
        flag = (sub == 0).astype(jnp.int32).reshape(1)
        tokens = features[:, :half]
        pieces = [features[b * BLOCK : (b + n) * BLOCK, half:] for b, n in runs]
    own = (q_weight, k_weight, v_weight)
    other = swapped(k_weight, "sub"), swapped(v_weight, "sub")
    other = (swapped(q_weight, "sub"),) + other
    wqa, wkva, wqb, wkvb = stage(flag, own, other)
    qb = q_bias[None, :]
    kvb = jnp.concatenate([jnp.zeros_like(v_bias), v_bias])[None, :]
    positions = (shard * rows + jnp.arange(rows, dtype=jnp.int32)).astype(jnp.float32)
    cos, sin = rotary_tables(positions)

    far_steps = [s for s in (1, 2, 4, 8) if s < n_ctx]
    queries, sources = {}, {}
    deps = ()

    def keys_values(i, deps):
        (b, n), piece = runs[i], pieces[i]
        kv = project(tokens, b * BLOCK, piece, wkva, wkvb, kvb, cos, sin, 2 * kvl * HD, kvl, deps)
        held = {"own": kv}
        held["prev"] = shifted(kv, ("ctx", "sub"), 1)
        for s in far_steps:
            held["far", s] = shifted(kv, "ctx", 1) if s == 1 else shifted(held["far", s // 2], "ctx", s // 2)
        for r in range(n):
            for name, array in held.items():
                sources[name, b + r] = (array, r)
        return (kv,)

    def all_queries(i, deps):
        (b, n), piece = runs[i], pieces[i]
        tile = 2 * HD if q_weight.shape[1] % (2 * HD) == 0 else HD
        q = project(tokens, b * BLOCK, piece, wqa, wqb, qb, cos, sin, tile, tile // HD, deps)
        for r in range(n):
            queries[b + r] = (q, r)
        return (q,)

    mine = head.astype(jnp.int32).reshape(1)
    outs, results = {}, []

    def attention(pair, deps):
        arrays, plan, distances = [], [], []
        for b in pair:
            slots = []
            wanted = [(d, ("own", b - d) if d <= b else ("prev", blocks + b - d)) for d in NEAR + (blocks,)]
            wanted += [(n_sub * blocks * s, (("far", s), b)) for s in far_steps]
            for d, key in wanted:
                array, r = sources[key]
                at = next((i for i, a in enumerate(arrays) if a is array), None)
                if at is None:
                    at = len(arrays)
                    arrays.append(array)
                slots.append((at, r))
                distances.append(b - d)
            plan.append(tuple(slots))
        valid = shard * blocks + jnp.array(distances, jnp.int32) >= 0
        bias = jnp.where(valid, 0.0, -1e30).astype(jnp.float32)
        own = attend(bias, [queries[b] for b in pair], arrays, plan, kvl, deps)
        if paired:
            results.append((pair, own, swapped(own, "head")))
        else:
            for i, b in enumerate(pair):
                outs[b] = own[i * BLOCK : (i + 1) * BLOCK]
        return (own,)

    def together(i):
        b, n = runs[i]
        return tuple(range(b, b + n))

    deps = keys_values(0, deps)
    deps = all_queries(0, deps)
    deps = keys_values(1, deps)
    deps = all_queries(1, deps)
    deps = keys_values(2, deps)
    deps = attention(together(0), deps)
    deps = all_queries(2, deps)
    deps = keys_values(3, deps)
    deps = all_queries(3, deps)
    deps = attention(together(2), deps)
    deps = attention(together(1), deps)
    deps = attention(together(3), deps)
    if not paired:
        local = jnp.concatenate([outs[b] for b in range(blocks)], 0)
        return lax.all_gather(local, "head", axis=1, tiled=True)
    shape = (rows, n_head * q_weight.shape[1])
    total = None
    for pair, own, _ in results:
        total = place(total, own, mine, pair, shape)
    for pair, _, other in results:
        total = place(total, other, 1 - mine, pair, shape)
    return total


def solution(mesh):
    return jax.shard_map(
        layer,
        mesh=mesh,
        in_specs=(
            P(("groups", "ctx", "sub"), "head"),
            P("sub", "head"),
            P("sub", "head"),
            P("sub", "head"),
            P("head"),
            P("head"),
        ),
        out_specs=P(("groups", "ctx", "sub"), None),
        check_vma=False,
    )
```

profile of v0, /device:TPU:0, one launch (start us, length us, event | category | flops | bytes accessed | tf_op | source)
XLA Modules:
  0.0 187.8 jit_solution(10282792820927931464)
XLA Ops:
  1.0 2.0 %copy-done = bf16[1024,1792]{1,0:T(8,128)(2,1)S(1)} copy-done((bf16[1024,1792]{1,0:T(8,128)(2,1)S(1)}, bf16[1024,1792]{1,0:T(8,128)(2,1)}, u32[]{:S(2)}) %copy-start) | copy-done | bytes 3670040
  4.3 2.6 %collective-permute-start.5 = (bf16[256,1792]{1,0:T(8,128)(2,1)}, bf16[256,1792]{1,0:T(8,128)(2,1)S(1)}, u32[]{:S(2)}, u32[]{:S(2)}) collective-permute-start(bf16[256,1792]{1,0:T(8,128)(2,1)} %cut.6), channel_id=1, source_target_pairs={{0,2},{2,0},{1,3},{3,1},{4,6},{6,4},{5,7},{7,5},{8,10},{10,8},{9,1... | collective-permute-start | bytes 2752520 | tf_op jit(solution)/shard_map/ppermute | solution.py:26
  14.7 2.0 %collective-permute-start.4 = (bf16[256,1792]{1,0:T(8,128)(2,1)}, bf16[256,1792]{1,0:T(8,128)(2,1)S(1)}, u32[]{:S(2)}, u32[]{:S(2)}) collective-permute-start(bf16[256,1792]{1,0:T(8,128)(2,1)} %copy-done.7), channel_id=1, source_target_pairs={{0,2},{2,0},{1,3},{3,1},{4,6},{6,4},{5,7},{7,5},{8,10},{10,8},{9,1... | collective-permute-start | bytes 2752520 | tf_op jit(solution)/shard_map/ppermute | solution.py:26
  17.2 2.8 %copy-done.3 = bf16[1792,1792]{1,0:T(8,128)(2,1)S(1)} copy-done((bf16[1792,1792]{1,0:T(8,128)(2,1)S(1)}, bf16[1792,1792]{1,0:T(8,128)(2,1)}, u32[]{:S(2)}) %copy-start.3) | copy-done | bytes 6422552
  21.2 4.4 %stage.1 = (bf16[1792,1792]{1,0:T(8,128)(2,1)S(1)}, bf16[1792,512]{1,0:T(8,128)(2,1)S(1)}, bf16[1792,1792]{1,0:T(8,128)(2,1)S(1)}, bf16[1792,512]{1,0:T(8,128)(2,1)S(1)}) custom-call(s32[1]{0:T(128)} %bitcast.1.flag, bf16[1792,1792]{1,0:T(8,128)(2,1)S(1)} %copy-done.3, bf16[1792,256]{1,0:T(8,128)(2,1)S(1)} %copy-done.4, bf16[1792,256]{1,0:T(8,128)(2,1)S(1)} %copy-done.5, ...), custom_call_target="tpu_custom_call" | custom-call | bytes 16515072 | tf_op jit(solution)/shard_map/stage/pallas_call | solution.py:77
  25.6 2.7 %collective-permute-done.5.tb = bf16[256,1792]{1,0:T(8,128)(2,1)S(1)} collective-permute-done((bf16[256,1792]{1,0:T(8,128)(2,1)}, bf16[256,1792]{1,0:T(8,128)(2,1)S(1)}, u32[]{:S(2)}, u32[]{:S(2)}) %collective-permute-start.5) | collective-permute-done | bytes 917536 | tf_op jit(solution)/shard_map/ppermute | solution.py:26
  29.6 2.2 %collective-permute-start.8 = (bf16[256,512]{1,0:T(8,128)(2,1)S(1)}, bf16[256,512]{1,0:T(8,128)(2,1)S(1)}, u32[]{:S(2)}, u32[]{:S(2)}) collective-permute-start(bf16[256,512]{1,0:T(8,128)(2,1)S(1)} %shard_map.100.refs_0_.refs_2_.refs_3_), channel_id=1, source_target_pairs={{0,4},{4,8},{8,12},{12,0},{1,5},{5,9},{9,13},{13,1},{2,6},{6,10},{... | collective-permute-start | bytes 786440 | tf_op jit(solution)/shard_map/ppermute | solution.py:22
  31.8 5.0 %shard_map.101.refs_0_.refs_1_ = bf16[256,1792]{1,0:T(8,128)(2,1)S(1)} custom-call(bf16[1024,1792]{1,0:T(8,128)(2,1)S(1)} %copy-done.2, bf16[256,1792]{1,0:T(8,128)(2,1)S(1)} %collective-permute-done.5.tb, bf16[1792,1792]{1,0:T(8,128)(2,1)S(1)} %get-tuple-element.9.wa, bf16[1792,1792]{1,0:T(8,128)(2,1)S(1)} %get-tuple-element.10.wb, ...), custom_call_target="tpu_custom_call" | custom-call | flops 3288334336 | tf_op jit(solution)/shard_map/pallas_call | solution.py:116
  36.8 11.2 %collective-permute-done.6.tb = bf16[256,1792]{1,0:T(8,128)(2,1)S(1)} collective-permute-done((bf16[256,1792]{1,0:T(8,128)(2,1)}, bf16[256,1792]{1,0:T(8,128)(2,1)S(1)}, u32[]{:S(2)}, u32[]{:S(2)}) %collective-permute-start.6) | collective-permute-done | bytes 917536 | tf_op jit(solution)/shard_map/ppermute | solution.py:26
  49.2 2.2 %collective-permute-start.14 = (bf16[256,512]{1,0:T(8,128)(2,1)S(1)}, bf16[256,512]{1,0:T(8,128)(2,1)S(1)}, u32[]{:S(2)}, u32[]{:S(2)}) collective-permute-start(bf16[256,512]{1,0:T(8,128)(2,1)S(1)} %shard_map.102.refs_0_.refs_4_.refs_3_.refs_2_), channel_id=1, source_target_pairs={{0,4},{4,8},{8,12},{12,0},{1,5},{5,9},{9,13},{13,1},{2,6},{6,10},{... | collective-permute-start | bytes 786440 | tf_op jit(solution)/shard_map/ppermute | solution.py:22
  51.4 5.0 %shard_map.103.refs_0_.refs_1_ = bf16[256,1792]{1,0:T(8,128)(2,1)S(1)} custom-call(bf16[1024,1792]{1,0:T(8,128)(2,1)S(1)} %copy-done.2, bf16[256,1792]{1,0:T(8,128)(2,1)S(1)} %collective-permute-done.6.tb, bf16[1792,1792]{1,0:T(8,128)(2,1)S(1)} %get-tuple-element.9.wa, bf16[1792,1792]{1,0:T(8,128)(2,1)S(1)} %get-tuple-element.10.wb, ...), custom_call_target="tpu_custom_call" | custom-call | flops 3288334336 | tf_op jit(solution)/shard_map/pallas_call | solution.py:116
  56.4 11.3 %collective-permute-done.4.tb = bf16[256,1792]{1,0:T(8,128)(2,1)S(1)} collective-permute-done((bf16[256,1792]{1,0:T(8,128)(2,1)}, bf16[256,1792]{1,0:T(8,128)(2,1)S(1)}, u32[]{:S(2)}, u32[]{:S(2)}) %collective-permute-start.4) | collective-permute-done | bytes 917536 | tf_op jit(solution)/shard_map/ppermute | solution.py:26
  68.9 2.2 %collective-permute-start.17 = (bf16[256,512]{1,0:T(8,128)(2,1)S(1)}, bf16[256,512]{1,0:T(8,128)(2,1)S(1)}, u32[]{:S(2)}, u32[]{:S(2)}) collective-permute-start(bf16[256,512]{1,0:T(8,128)(2,1)S(1)} %shard_map.104.refs_3_.refs_8_.refs_2_.refs_4_), channel_id=1, source_target_pairs={{0,4},{4,8},{8,12},{12,0},{1,5},{5,9},{9,13},{13,1},{2,6},{6,10},{... | collective-permute-start | bytes 786440 | tf_op jit(solution)/shard_map/ppermute | solution.py:22
  74.4 5.8 %collective-permute-done.17.refs_6_ = bf16[256,512]{1,0:T(8,128)(2,1)S(1)} collective-permute-done((bf16[256,512]{1,0:T(8,128)(2,1)S(1)}, bf16[256,512]{1,0:T(8,128)(2,1)S(1)}, u32[]{:S(2)}, u32[]{:S(2)}) %collective-permute-start.17) | collective-permute-done | bytes 262176 | tf_op jit(solution)/shard_map/ppermute | solution.py:22
  80.2 5.6 %collective-permute-done.9.refs_7_ = bf16[256,512]{1,0:T(8,128)(2,1)S(1)} collective-permute-done((bf16[256,512]{1,0:T(8,128)(2,1)S(1)}, bf16[256,512]{1,0:T(8,128)(2,1)S(1)}, u32[]{:S(2)}, u32[]{:S(2)}) %collective-permute-start.9) | collective-permute-done | bytes 262176 | tf_op jit(solution)/shard_map/ppermute | solution.py:22
  85.8 6.0 %attend.4.refs_0_.src = bf16[256,1792]{1,0:T(8,128)(2,1)S(1)} custom-call(f32[14]{0:T(128)S(1)} %compare_select_fusion.2.bias, bf16[256,1792]{1,0:T(8,128)(2,1)S(1)} %shard_map.101.refs_0_.refs_1_, bf16[256,1792]{1,0:T(8,128)(2,1)S(1)} %shard_map.101.refs_0_.refs_1_, bf16[256,512]{1,0:T(8,128)(2,1)S(1)} %shard_map.100.refs_0_.refs_2_.refs_3_, ...), custom_call_target="tpu_custom_call" | custom-call | flops 3288334336 | tf_op jit(solution)/shard_map/attend/pallas_call | solution.py:169
  91.9 5.0 %shard_map.105.refs_0_.refs_1_ = bf16[256,1792]{1,0:T(8,128)(2,1)S(1)} custom-call(bf16[1024,1792]{1,0:T(8,128)(2,1)S(1)} %copy-done.2, bf16[256,1792]{1,0:T(8,128)(2,1)S(1)} %collective-permute-done.4.tb, bf16[1792,1792]{1,0:T(8,128)(2,1)S(1)} %get-tuple-element.9.wa, bf16[1792,1792]{1,0:T(8,128)(2,1)S(1)} %get-tuple-element.10.wb, ...), custom_call_target="tpu_custom_call" | custom-call | flops 3288334336 | tf_op jit(solution)/shard_map/pallas_call | solution.py:116
  98.2 5.0 %shard_map.107.refs_8_.refs_0_.refs_1_ = bf16[256,1792]{1,0:T(8,128)(2,1)S(1)} custom-call(bf16[1024,1792]{1,0:T(8,128)(2,1)S(1)} %copy-done.2, bf16[256,1792]{1,0:T(8,128)(2,1)S(1)} %collective-permute-done.tb, bf16[1792,1792]{1,0:T(8,128)(2,1)S(1)} %get-tuple-element.9.wa, bf16[1792,1792]{1,0:T(8,128)(2,1)S(1)} %get-tuple-element.10.wb, ...), custom_call_target="tpu_custom_call" | custom-call | flops 3288334336 | tf_op jit(solution)/shard_map/pallas_call | solution.py:116
  106.5 6.1 %attend.5.refs_8_.src = bf16[256,1792]{1,0:T(8,128)(2,1)S(1)} custom-call(f32[14]{0:T(128)S(1)} %compare_select_fusion.bias, bf16[256,1792]{1,0:T(8,128)(2,1)S(1)} %shard_map.105.refs_0_.refs_1_, bf16[256,1792]{1,0:T(8,128)(2,1)S(1)} %shard_map.105.refs_0_.refs_1_, bf16[256,512]{1,0:T(8,128)(2,1)S(1)} %shard_map.104.refs_3_.refs_8_.refs_2_.refs_4_, ...), custom_call_target="tpu_custom_call" | custom-call | flops 3288334336 | tf_op jit(solution)/shard_map/attend/pallas_call | solution.py:169
  114.8 6.1 %attend.6.refs_8_.src = bf16[256,1792]{1,0:T(8,128)(2,1)S(1)} custom-call(f32[14]{0:T(128)S(1)} %compare_select_fusion.1.bias, bf16[256,1792]{1,0:T(8,128)(2,1)S(1)} %shard_map.103.refs_0_.refs_1_, bf16[256,1792]{1,0:T(8,128)(2,1)S(1)} %shard_map.103.refs_0_.refs_1_, bf16[256,512]{1,0:T(8,128)(2,1)S(1)} %shard_map.102.refs_0_.refs_4_.refs_3_.refs_2_, ...), custom_call_target="tpu_custom_call" | custom-call | flops 3288334336 | tf_op jit(solution)/shard_map/attend/pallas_call | solution.py:169
  124.3 6.0 %attend.7.src = bf16[256,1792]{1,0:T(8,128)(2,1)S(1)} custom-call(f32[14]{0:T(128)S(1)} %compare_select_fusion.3.bias, bf16[256,1792]{1,0:T(8,128)(2,1)S(1)} %shard_map.107.refs_8_.refs_0_.refs_1_, bf16[256,1792]{1,0:T(8,128)(2,1)S(1)} %shard_map.107.refs_8_.refs_0_.refs_1_, bf16[256,512]{1,0:T(8,128)(2,1)S(1)} %shard_map.106.refs_0_.refs_2_, ...), custom_call_target="tpu_custom_call" | custom-call | flops 3288334336 | tf_op jit(solution)/shard_map/attend/pallas_call | solution.py:169
  136.8 10.7 %collective-permute-done.21.src = bf16[256,1792]{1,0:T(8,128)(2,1)S(1)} collective-permute-done((bf16[256,1792]{1,0:T(8,128)(2,1)S(1)}, bf16[256,1792]{1,0:T(8,128)(2,1)S(1)}, u32[]{:S(2)}, u32[]{:S(2)}) %collective-permute-start.21) | collective-permute-done | bytes 917536 | tf_op jit(solution)/shard_map/ppermute | solution.py:26
  148.4 18.7 %collective-permute-done.20.src = bf16[256,1792]{1,0:T(8,128)(2,1)S(1)} collective-permute-done((bf16[256,1792]{1,0:T(8,128)(2,1)S(1)}, bf16[256,1792]{1,0:T(8,128)(2,1)S(1)}, u32[]{:S(2)}, u32[]{:S(2)}) %collective-permute-start.20) | collective-permute-done | bytes 917536 | tf_op jit(solution)/shard_map/ppermute | solution.py:26
  168.1 18.7 %collective-permute-done.19.src = bf16[256,1792]{1,0:T(8,128)(2,1)S(1)} collective-permute-done((bf16[256,1792]{1,0:T(8,128)(2,1)S(1)}, bf16[256,1792]{1,0:T(8,128)(2,1)S(1)}, u32[]{:S(2)}, u32[]{:S(2)}) %collective-permute-start.19) | collective-permute-done | bytes 917536 | tf_op jit(solution)/shard_map/ppermute | solution.py:26
  (85 shorter events, 38.0 us)
Async XLA Ops:
  0.0 17.2 %collective-permute-start.1 = (bf16[1792,1792]{1,0:T(8,128)(2,1)}, bf16[1792,1792]{1,0:T(8,128)(2,1)}, u32[]{:S(2)}, u32[]{:S(2)}) collective-permute-start(bf16[1792,1792]{1,0:T(8,128)(2,1)} %refs_0_.1), channel_id=1, source_target_pairs={{0,1},{1,0},{2,3},{3,2},{4,5},{5,4},{6,7},{7,6},{8,9},{9,8},{10,11... | collective-permute-start | bytes 19267592 | tf_op jit(solution)/shard_map/ppermute | solution.py:26
  0.5 14.2 %collective-permute-start.2 = (bf16[1792,256]{1,0:T(8,128)(2,1)}, bf16[1792,256]{1,0:T(8,128)(2,1)}, u32[]{:S(2)}, u32[]{:S(2)}) collective-permute-start(bf16[1792,256]{1,0:T(8,128)(2,1)} %refs_1_.1), channel_id=1, source_target_pairs={{0,1},{1,0},{2,3},{3,2},{4,5},{5,4},{6,7},{7,6},{8,9},{9,8},{10,11... | collective-permute-start | bytes 2752520 | tf_op jit(solution)/shard_map/ppermute | solution.py:26
  0.6 16.5 %collective-permute-start.3 = (bf16[1792,256]{1,0:T(8,128)(2,1)}, bf16[1792,256]{1,0:T(8,128)(2,1)}, u32[]{:S(2)}, u32[]{:S(2)}) collective-permute-start(bf16[1792,256]{1,0:T(8,128)(2,1)} %refs_2_.1), channel_id=1, source_target_pairs={{0,1},{1,0},{2,3},{3,2},{4,5},{5,4},{6,7},{7,6},{8,9},{9,8},{10,11... | collective-permute-start | bytes 2752520 | tf_op jit(solution)/shard_map/ppermute | solution.py:26
  4.3 24.0 %collective-permute-start.5 = (bf16[256,1792]{1,0:T(8,128)(2,1)}, bf16[256,1792]{1,0:T(8,128)(2,1)S(1)}, u32[]{:S(2)}, u32[]{:S(2)}) collective-permute-start(bf16[256,1792]{1,0:T(8,128)(2,1)} %cut.6), channel_id=1, source_target_pairs={{0,2},{2,0},{1,3},{3,1},{4,6},{6,4},{5,7},{7,5},{8,10},{10,8},{9,1... | collective-permute-start | bytes 2752520 | tf_op jit(solution)/shard_map/ppermute | solution.py:26
  8.2 39.8 %collective-permute-start.6 = (bf16[256,1792]{1,0:T(8,128)(2,1)}, bf16[256,1792]{1,0:T(8,128)(2,1)S(1)}, u32[]{:S(2)}, u32[]{:S(2)}) collective-permute-start(bf16[256,1792]{1,0:T(8,128)(2,1)} %cut.7), channel_id=1, source_target_pairs={{0,2},{2,0},{1,3},{3,1},{4,6},{6,4},{5,7},{7,5},{8,10},{10,8},{9,1... | collective-permute-start | bytes 2752520 | tf_op jit(solution)/shard_map/ppermute | solution.py:26
  14.7 53.0 %collective-permute-start.4 = (bf16[256,1792]{1,0:T(8,128)(2,1)}, bf16[256,1792]{1,0:T(8,128)(2,1)S(1)}, u32[]{:S(2)}, u32[]{:S(2)}) collective-permute-start(bf16[256,1792]{1,0:T(8,128)(2,1)} %copy-done.7), channel_id=1, source_target_pairs={{0,2},{2,0},{1,3},{3,1},{4,6},{6,4},{5,7},{7,5},{8,10},{10,8},{9,1... | collective-permute-start | bytes 2752520 | tf_op jit(solution)/shard_map/ppermute | solution.py:26
  17.1 79.8 %collective-permute-start = (bf16[256,1792]{1,0:T(8,128)(2,1)}, bf16[256,1792]{1,0:T(8,128)(2,1)S(1)}, u32[]{:S(2)}, u32[]{:S(2)}) collective-permute-start(bf16[256,1792]{1,0:T(8,128)(2,1)} %copy-done.6), channel_id=1, source_target_pairs={{0,2},{2,0},{1,3},{3,1},{4,6},{6,4},{5,7},{7,5},{8,10},{10,8},{9,1... | collective-permute-start | bytes 2752520 | tf_op jit(solution)/shard_map/ppermute | solution.py:26
  29.5 43.1 %collective-permute-start.7 = (bf16[256,512]{1,0:T(8,128)(2,1)S(1)}, bf16[256,512]{1,0:T(8,128)(2,1)S(1)}, u32[]{:S(2)}, u32[]{:S(2)}) collective-permute-start(bf16[256,512]{1,0:T(8,128)(2,1)S(1)} %shard_map.100.refs_0_.refs_2_.refs_3_), channel_id=1, source_target_pairs={{0,1},{1,4},{4,5},{5,8},{8,9},{9,12},{12,13},{13,0},{2,3},{3,6},{6... | collective-permute-start | bytes 786440 | tf_op jit(solution)/shard_map/ppermute | solution.py:22
  29.6 41.4 %collective-permute-start.8 = (bf16[256,512]{1,0:T(8,128)(2,1)S(1)}, bf16[256,512]{1,0:T(8,128)(2,1)S(1)}, u32[]{:S(2)}, u32[]{:S(2)}) collective-permute-start(bf16[256,512]{1,0:T(8,128)(2,1)S(1)} %shard_map.100.refs_0_.refs_2_.refs_3_), channel_id=1, source_target_pairs={{0,4},{4,8},{8,12},{12,0},{1,5},{5,9},{9,13},{13,1},{2,6},{6,10},{... | collective-permute-start | bytes 786440 | tf_op jit(solution)/shard_map/ppermute | solution.py:22
  49.2 23.5 %collective-permute-start.14 = (bf16[256,512]{1,0:T(8,128)(2,1)S(1)}, bf16[256,512]{1,0:T(8,128)(2,1)S(1)}, u32[]{:S(2)}, u32[]{:S(2)}) collective-permute-start(bf16[256,512]{1,0:T(8,128)(2,1)S(1)} %shard_map.102.refs_0_.refs_4_.refs_3_.refs_2_), channel_id=1, source_target_pairs={{0,4},{4,8},{8,12},{12,0},{1,5},{5,9},{9,13},{13,1},{2,6},{6,10},{... | collective-permute-start | bytes 786440 | tf_op jit(solution)/shard_map/ppermute | solution.py:22
  56.4 16.2 %copy-start.11 = (s32[14]{0:T(128)S(1)}, s32[14]{0:T(128)}, u32[]{:S(2)}) copy-start(s32[14]{0:T(128)} %constant.43.clone) | copy-start | bytes 172
  68.9 11.3 %collective-permute-start.17 = (bf16[256,512]{1,0:T(8,128)(2,1)S(1)}, bf16[256,512]{1,0:T(8,128)(2,1)S(1)}, u32[]{:S(2)}, u32[]{:S(2)}) collective-permute-start(bf16[256,512]{1,0:T(8,128)(2,1)S(1)} %shard_map.104.refs_3_.refs_8_.refs_2_.refs_4_), channel_id=1, source_target_pairs={{0,4},{4,8},{8,12},{12,0},{1,5},{5,9},{9,13},{13,1},{2,6},{6,10},{... | collective-permute-start | bytes 786440 | tf_op jit(solution)/shard_map/ppermute | solution.py:22
  71.0 14.8 %collective-permute-start.9 = (bf16[256,512]{1,0:T(8,128)(2,1)S(1)}, bf16[256,512]{1,0:T(8,128)(2,1)S(1)}, u32[]{:S(2)}, u32[]{:S(2)}) collective-permute-start(bf16[256,512]{1,0:T(8,128)(2,1)S(1)} %collective-permute-done.8.refs_6_), channel_id=1, source_target_pairs={{0,4},{4,8},{8,12},{12,0},{1,5},{5,9},{9,13},{13,1},{2,6},{6,10},{... | collective-permute-start | bytes 786440 | tf_op jit(solution)/shard_map/ppermute | solution.py:22
  72.6 42.1 %collective-permute-start.13 = (bf16[256,512]{1,0:T(8,128)(2,1)S(1)}, bf16[256,512]{1,0:T(8,128)(2,1)S(1)}, u32[]{:S(2)}, u32[]{:S(2)}) collective-permute-start(bf16[256,512]{1,0:T(8,128)(2,1)S(1)} %shard_map.102.refs_0_.refs_4_.refs_3_.refs_2_), channel_id=1, source_target_pairs={{0,1},{1,4},{4,5},{5,8},{8,9},{9,12},{12,13},{13,0},{2,3},{3,6},{6... | collective-permute-start | bytes 786440 | tf_op jit(solution)/shard_map/ppermute | solution.py:22
  72.7 30.5 %collective-permute-start.16 = (bf16[256,512]{1,0:T(8,128)(2,1)S(1)}, bf16[256,512]{1,0:T(8,128)(2,1)S(1)}, u32[]{:S(2)}, u32[]{:S(2)}) collective-permute-start(bf16[256,512]{1,0:T(8,128)(2,1)S(1)} %shard_map.104.refs_3_.refs_8_.refs_2_.refs_4_), channel_id=1, source_target_pairs={{0,1},{1,4},{4,5},{5,8},{8,9},{9,12},{12,13},{13,0},{2,3},{3,6},{6... | collective-permute-start | bytes 786440 | tf_op jit(solution)/shard_map/ppermute | solution.py:22
  80.2 34.6 %collective-permute-start.15 = (bf16[256,512]{1,0:T(8,128)(2,1)S(1)}, bf16[256,512]{1,0:T(8,128)(2,1)S(1)}, u32[]{:S(2)}, u32[]{:S(2)}) collective-permute-start(bf16[256,512]{1,0:T(8,128)(2,1)S(1)} %collective-permute-done.14.refs_6_), channel_id=1, source_target_pairs={{0,4},{4,8},{8,12},{12,0},{1,5},{5,9},{9,13},{13,1},{2,6},{6,10},{... | collective-permute-start | bytes 786440 | tf_op jit(solution)/shard_map/ppermute | solution.py:22
  85.8 19.2 %collective-permute-start.18 = (bf16[256,512]{1,0:T(8,128)(2,1)S(1)}, bf16[256,512]{1,0:T(8,128)(2,1)S(1)}, u32[]{:S(2)}, u32[]{:S(2)}) collective-permute-start(bf16[256,512]{1,0:T(8,128)(2,1)S(1)} %collective-permute-done.17.refs_6_), channel_id=1, source_target_pairs={{0,4},{4,8},{8,12},{12,0},{1,5},{5,9},{9,13},{13,1},{2,6},{6,10},{... | collective-permute-start | bytes 786440 | tf_op jit(solution)/shard_map/ppermute | solution.py:22
  98.1 8.4 %collective-permute-start.10 = (bf16[256,512]{1,0:T(8,128)(2,1)S(1)}, bf16[256,512]{1,0:T(8,128)(2,1)S(1)}, u32[]{:S(2)}, u32[]{:S(2)}) collective-permute-start(bf16[256,512]{1,0:T(8,128)(2,1)S(1)} %shard_map.106.refs_0_.refs_2_), channel_id=1, source_target_pairs={{0,1},{1,4},{4,5},{5,8},{8,9},{9,12},{12,13},{13,0},{2,3},{3,6},{6... | collective-permute-start | bytes 786440 | tf_op jit(solution)/shard_map/ppermute | solution.py:22
  103.2 10.5 %collective-permute-start.11 = (bf16[256,512]{1,0:T(8,128)(2,1)S(1)}, bf16[256,512]{1,0:T(8,128)(2,1)S(1)}, u32[]{:S(2)}, u32[]{:S(2)}) collective-permute-start(bf16[256,512]{1,0:T(8,128)(2,1)S(1)} %shard_map.106.refs_0_.refs_2_), channel_id=1, source_target_pairs={{0,4},{4,8},{8,12},{12,0},{1,5},{5,9},{9,13},{13,1},{2,6},{6,10},{... | collective-permute-start | bytes 786440 | tf_op jit(solution)/shard_map/ppermute | solution.py:22
  105.0 30.9 %collective-permute-start.22 = (bf16[256,1792]{1,0:T(8,128)(2,1)S(1)}, bf16[256,1792]{1,0:T(8,128)(2,1)S(1)}, u32[]{:S(2)}, u32[]{:S(2)}) collective-permute-start(bf16[256,1792]{1,0:T(8,128)(2,1)S(1)} %attend.4.refs_0_.src), channel_id=1, source_target_pairs={{0,2},{2,0},{1,3},{3,1},{4,6},{6,4},{5,7},{7,5},{8,10},{10,8},{9,1... | collective-permute-start | bytes 2752520 | tf_op jit(solution)/shard_map/ppermute | solution.py:26
  112.6 34.9 %collective-permute-start.21 = (bf16[256,1792]{1,0:T(8,128)(2,1)S(1)}, bf16[256,1792]{1,0:T(8,128)(2,1)S(1)}, u32[]{:S(2)}, u32[]{:S(2)}) collective-permute-start(bf16[256,1792]{1,0:T(8,128)(2,1)S(1)} %attend.5.refs_8_.src), channel_id=1, source_target_pairs={{0,2},{2,0},{1,3},{3,1},{4,6},{6,4},{5,7},{7,5},{8,10},{10,8},{9,1... | collective-permute-start | bytes 2752520 | tf_op jit(solution)/shard_map/ppermute | solution.py:26
  113.7 10.5 %collective-permute-start.12 = (bf16[256,512]{1,0:T(8,128)(2,1)S(1)}, bf16[256,512]{1,0:T(8,128)(2,1)S(1)}, u32[]{:S(2)}, u32[]{:S(2)}) collective-permute-start(bf16[256,512]{1,0:T(8,128)(2,1)S(1)} %collective-permute-done.11.refs_6_), channel_id=1, source_target_pairs={{0,4},{4,8},{8,12},{12,0},{1,5},{5,9},{9,13},{13,1},{2,6},{6,10},{... | collective-permute-start | bytes 786440 | tf_op jit(solution)/shard_map/ppermute | solution.py:22
  120.8 46.3 %collective-permute-start.20 = (bf16[256,1792]{1,0:T(8,128)(2,1)S(1)}, bf16[256,1792]{1,0:T(8,128)(2,1)S(1)}, u32[]{:S(2)}, u32[]{:S(2)}) collective-permute-start(bf16[256,1792]{1,0:T(8,128)(2,1)S(1)} %attend.6.refs_8_.src), channel_id=1, source_target_pairs={{0,2},{2,0},{1,3},{3,1},{4,6},{6,4},{5,7},{7,5},{8,10},{10,8},{9,1... | collective-permute-start | bytes 2752520 | tf_op jit(solution)/shard_map/ppermute | solution.py:26
  130.3 56.5 %collective-permute-start.19 = (bf16[256,1792]{1,0:T(8,128)(2,1)S(1)}, bf16[256,1792]{1,0:T(8,128)(2,1)S(1)}, u32[]{:S(2)}, u32[]{:S(2)}) collective-permute-start(bf16[256,1792]{1,0:T(8,128)(2,1)S(1)} %attend.7.src), channel_id=1, source_target_pairs={{0,2},{2,0},{1,3},{3,1},{4,6},{6,4},{5,7},{7,5},{8,10},{10,8},{9,1... | collective-permute-start | bytes 2752520 | tf_op jit(solution)/shard_map/ppermute | solution.py:26
  (13 other events, 76.9 us)
where the time goes:
time: 188 us
  waiting for transfers between devices  86.8 us (46%)
  Pallas kernels  64 us (34%)
  starting transfers between devices  24.4 us (13%)
  local copies, waits for them, and re-layouts  9.96 us (5%)
  other arithmetic  2.27 us (1%)
    ppermute x11, waiting for transfers between devices, swapped(): return lax.ppermute(value, axis, [(0, 1), (1, 0)])  73.3 us
    pallas_call x8, Pallas kernels, project(): pl.pallas_call(functools.partial(project_body, row, tile, rot), out_shape...  24.9 us
    pallas_call x4, Pallas kernels, attend(): pl.pallas_call(functools.partial(attend_body, plan, len(arrays), kvl), ou...  24.2 us
    ppermute x12, waiting for transfers between devices, shifted(): lax.ppermute(value, axis, [(s, (s + steps) % count) for s in range(count)])  13.5 us
    ppermute x12, starting transfers between devices, shifted(): lax.ppermute(value, axis, [(s, (s + steps) % count) for s in range(count)])  12.7 us
    ppermute x11, starting transfers between devices, swapped(): return lax.ppermute(value, axis, [(0, 1), (1, 0)])  11.7 us
    unnamed x28, local copies, waits for them, and re-layouts  9.94 us
    pallas_call x8, Pallas kernels, place(): pl.pallas_call(place_body, out_shape=jax.ShapeDtypeStruct(shape, jnp.bflo...  7.59 us
  transfers between devices with their start and end apart: 23, of which 10 were waited for; matrix products, arithmetic and copies ran while one was open for 1% of the time, Pallas kernels for 34%

commit v1 on v0

v1 whole, which is shorter than its diff:
```python
import functools
import math

import jax
import jax.numpy as jnp
from jax import lax
from jax.experimental import pallas as pl
from jax.experimental.pallas import tpu as pltpu
from jax.sharding import PartitionSpec as P


HQ = 28
KVH = 4
HD = 128
BLOCK = 128
NEAR = (0, 1, 2, 4)
GROUP = HQ // KVH
SHARED = 4


def shifted(value, axis, steps):
    count = lax.axis_size(axis)
    return lax.ppermute(value, axis, [(s, (s + steps) % count) for s in range(count)])


def swapped(value, axis):
    return lax.ppermute(value, axis, [(0, 1), (1, 0)])


def rotary_tables(positions):
    half = HD // 2
    freqs = jnp.exp(-(2.0 * jnp.arange(half, dtype=jnp.float32) / (2 * half)) * math.log(1000000.0))
    angle = positions[:, None] * freqs[None, :]
    cosine = jnp.cos(angle)
    sine = jnp.sin(angle)
    return jnp.concatenate([cosine, cosine], 1), jnp.concatenate([-sine, sine], 1)


VMEM = pl.BlockSpec(memory_space=pltpu.VMEM)
SMEM = pl.BlockSpec(memory_space=pltpu.SMEM)
ANY = pl.BlockSpec(memory_space=pl.ANY)
HBM = pl.BlockSpec(memory_space=pltpu.HBM)


def params(mib):
    return pltpu.CompilerParams(vmem_limit_bytes=mib * 2**20)


def stage_body(n, flag, *refs):
    own, other, outs, sems = refs[:n], refs[n : 2 * n], refs[-5:-1], refs[-1]

    def bring(first, second):
        copies = []
        for half, sources in enumerate((first, second)):
            q_out, kv_out = outs[2 * half], outs[2 * half + 1]
            nk = sources[1].shape[1]
            targets = (q_out, kv_out.at[:, pl.ds(0, nk)], kv_out.at[:, pl.ds(nk, nk)])
            for i, (source, target) in enumerate(zip(sources, targets)):
                copies.append(pltpu.make_async_copy(source, target, sems.at[half, i]))
        for copy in copies:
            copy.start()
        for copy in copies:
            copy.wait()

    @pl.when(flag[0] == 1)
    def _():
        bring(own, other)

    @pl.when(flag[0] != 1)
    def _():
        bring(other, own)


def stage(flag, own, other, deps):
    half, nq = own[0].shape
    nk = own[1].shape[1]
    shapes = [pltpu.VMEM((half, nq), jnp.bfloat16), pltpu.VMEM((half, 2 * nk), jnp.bfloat16)] * 2
    return pl.pallas_call(
        functools.partial(stage_body, len(own)),
        out_shape=tuple(shapes),
        in_specs=[SMEM] + [HBM] * (2 * len(own)) + [ANY] * len(deps),
        out_specs=(VMEM,) * 4,
        scratch_shapes=[pltpu.SemaphoreType.DMA((2, len(own)))],
        compiler_params=params(2),
        cost_estimate=pl.CostEstimate(flops=0, bytes_accessed=4 * half * (nq + 2 * nk), transcendentals=0),
        name="stage",
    )(flag, *own, *other, *deps)


def project_body(row, tile, rot, ta, tb, wa, wb, bias, cos, sin, *refs):
    out = refs[-1]
    rows = tb.shape[0]
    mine = pl.ds(row, rows)

    def columns(i):
        at = pl.ds(pl.multiple_of(i * tile, tile), tile)
        acc = jnp.dot(ta[mine, :], wa[:, at], preferred_element_type=jnp.float32)
        acc = acc + jnp.dot(tb[...], wb[:, at], preferred_element_type=jnp.float32)
        acc = acc + bias[:, at]
        heads = []
        for h in range(tile // HD):
            v = acc[:, h * HD : (h + 1) * HD]
            if h < rot:
                v = v * cos[mine, :] + pltpu.roll(v, HD // 2, 1) * sin[mine, :]
            heads.append(v.astype(jnp.bfloat16))
        out[:, at] = jnp.concatenate(heads, 1)

    if tile == out.shape[1]:
        columns(0)
    else:
        pl.loop(0, out.shape[1] // tile)(columns)


def project(tokens, row, piece, wa, wb, bias, cos, sin, tile, rot, deps):
    rows, half = piece.shape
    cols = wa.shape[1]
    return pl.pallas_call(
        functools.partial(project_body, row, tile, rot),
        out_shape=jax.ShapeDtypeStruct((rows, cols), jnp.bfloat16),
        in_specs=[VMEM] * 7 + [ANY] * len(deps),
        out_specs=VMEM,
        compiler_params=params(5),
        cost_estimate=pl.CostEstimate(flops=4 * rows * half * cols, bytes_accessed=0, transcendentals=0),
    )(tokens, piece, wa, wb, bias, cos, sin, *deps)


def attend_body(plan, n_arrays, q_row, groups, per, v_base, n_sent, bias, query, *refs):
    arrays = refs[:n_arrays]
    held = refs[-1]
    outs = refs[n_arrays:-1][-2:] if n_sent < groups * per else refs[-2:-1]
    scale = math.log2(math.e) / math.sqrt(HD)
    lower = lax.broadcasted_iota(jnp.int32, (BLOCK, BLOCK), 0) >= lax.broadcasted_iota(
        jnp.int32, (BLOCK, BLOCK), 1
    )
    rows = lambda r: slice(r * BLOCK, (r + 1) * BLOCK)

    def kv_head(g):
        for j, slots in enumerate(plan):
            n = len(slots)
            k_at = pl.ds(pl.multiple_of(g * HD, HD), HD)
            v_at = pl.ds(pl.multiple_of(v_base + g * HD, HD), HD)
            keys = jnp.concatenate([arrays[a][rows(r), k_at] for a, r in slots], 0)
            vals = jnp.concatenate([arrays[a][rows(r), v_at] for a, r in slots], 0)
            vals = jnp.concatenate([vals, jnp.ones_like(vals)], 1)
            for h in range(per):
                at = pl.ds(pl.multiple_of((g * per + h) * HD, HD), HD)
                s = lax.dot_general(
                    query[rows(q_row + j), at], keys, (((1,), (1,)), ((), ())),
                    preferred_element_type=jnp.float32,
                )
                parts = [jnp.where(lower, s[:, :BLOCK], -1e30)]
                for t in range(1, n):
                    parts.append(s[:, t * BLOCK : (t + 1) * BLOCK] + bias[j * n + t])
                s = jnp.concatenate(parts, 1)
                peak = jnp.max(s, axis=1, keepdims=True)
                p = jnp.exp2((s - peak) * scale).astype(jnp.bfloat16)
                o = jnp.dot(p, vals, preferred_element_type=jnp.float32)
                held[rows(j), at] = (o[:, :HD] / o[:, HD:]).astype(jnp.bfloat16)

    if groups == 1:
        kv_head(0)
    else:
        pl.loop(0, groups)(kv_head)
    outs[0][...] = held[:, : n_sent * HD]
    if len(outs) > 1:
        outs[1][...] = held[:, n_sent * HD :]


def attend(bias, query, q_row, arrays, plan, groups, per, v_base, n_sent, deps):
    nb = len(plan)
    heads = groups * per
    keys = len(plan[0]) * BLOCK
    shapes = [jax.ShapeDtypeStruct((nb * BLOCK, n * HD), jnp.bfloat16) for n in (n_sent, heads - n_sent) if n]
    return pl.pallas_call(
        functools.partial(attend_body, plan, len(arrays), q_row, groups, per, v_base, n_sent),
        out_shape=tuple(shapes),
        in_specs=[SMEM] + [VMEM] * (1 + len(arrays)) + [ANY] * len(deps),
        out_specs=(VMEM,) * len(shapes),
        scratch_shapes=[pltpu.VMEM((nb * BLOCK, heads * HD), jnp.bfloat16)],
        compiler_params=params(5),
        cost_estimate=pl.CostEstimate(
            flops=4 * nb * heads * HD * keys * BLOCK,
            bytes_accessed=0,
            transcendentals=nb * BLOCK * heads * keys,
        ),
        name="attend",
    )(bias, query, *arrays, *deps)


def order_body(flag, own, other, first, second, sems):
    def bring(sources):
        copies = [
            pltpu.make_async_copy(source, target, sems.at[i])
            for i, (source, target) in enumerate(zip(sources, (first, second)))
        ]
        for copy in copies:
            copy.start()
        for copy in copies:
            copy.wait()

    @pl.when(flag[0] == 1)
    def _():
        bring((own, other))

    @pl.when(flag[0] != 1)
    def _():
        bring((other, own))


def order_halves(flag, own, other, deps):
    half = pltpu.VMEM(own.shape, own.dtype)
    return pl.pallas_call(
        lambda *refs: order_body(*refs[:3], *refs[-3:]),
        out_shape=(half, half),
        in_specs=[SMEM] + [HBM] * 2 + [ANY] * len(deps),
        out_specs=(VMEM, VMEM),
        scratch_shapes=[pltpu.SemaphoreType.DMA((2,))],
        compiler_params=params(2),
        cost_estimate=pl.CostEstimate(flops=0, bytes_accessed=4 * own.size, transcendentals=0),
        name="order_halves",
    )(flag, own, other, *deps)


def project_shared_body(bases, ta, *refs):
    n_pieces = len(bases)
    pieces = refs[:n_pieces]
    wa, wb, bias, cos, sin = refs[n_pieces : n_pieces + 5]
    out, kv_out = refs[-2:]
    rows = pieces[0].shape[0]
    for i, tb in enumerate(pieces):
        mine = slice(bases[i], bases[i] + rows)
        here = slice(i * rows, (i + 1) * rows)

        def columns(t, last):
            at = pl.ds(pl.multiple_of(t * 2 * HD, 2 * HD), 2 * HD)
            acc = jnp.dot(ta[mine, :], wa[:, at], preferred_element_type=jnp.float32)
            acc = acc + jnp.dot(tb[...], wb[:, at], preferred_element_type=jnp.float32)
            acc = acc + bias[:, at]
            heads = []
            for h in range(2):
                v = acc[:, h * HD : (h + 1) * HD]
                if not (last and h):
                    v = v * cos[mine, :] + pltpu.roll(v, HD // 2, 1) * sin[mine, :]
                heads.append(v.astype(jnp.bfloat16))
            return jnp.concatenate(heads, 1)

        for t in range(SHARED // 2):
            out[here, t * 2 * HD : (t + 1) * 2 * HD] = columns(t, False)
        kv_out[here, :] = columns(SHARED // 2, True)


def project_shared(tokens, bases, pieces, wa, wb, bias, cos, sin, deps):
    rows, half = pieces[0].shape
    total = rows * len(pieces)
    cols = wa.shape[1]
    return pl.pallas_call(
        functools.partial(project_shared_body, bases),
        out_shape=(
            jax.ShapeDtypeStruct((total, SHARED * HD), jnp.bfloat16),
            jax.ShapeDtypeStruct((total, 2 * HD), jnp.bfloat16),
        ),
        in_specs=[VMEM] * (len(pieces) + 6) + [ANY] * len(deps),
        out_specs=(VMEM, VMEM),
        compiler_params=params(5),
        cost_estimate=pl.CostEstimate(flops=4 * total * half * cols, bytes_accessed=0, transcendentals=0),
        name="project_shared",
    )(tokens, *pieces, wa, wb, bias, cos, sin, *deps)


def cut_weights_body(index, wq, wk, wv, out, sems):
    n = out.shape[0]
    rows = pl.ds(pl.multiple_of(index[0] * n, 16), n)
    width = SHARED * HD
    copies = [
        pltpu.make_async_copy(
            wq.at[rows, pl.ds(wq.shape[1] - width, width)], out.at[:, pl.ds(0, width)], sems.at[0]
        ),
        pltpu.make_async_copy(
            wk.at[rows, pl.ds(wk.shape[1] - HD, HD)], out.at[:, pl.ds(width, HD)], sems.at[1]
        ),
        pltpu.make_async_copy(
            wv.at[rows, pl.ds(wv.shape[1] - HD, HD)], out.at[:, pl.ds(width + HD, HD)], sems.at[2]
        ),
    ]
    for copy in copies:
        copy.start()
    for copy in copies:
        copy.wait()


def cut_weights(index, weights, parts):
    n = weights[0].shape[0] // parts
    cols = (SHARED + 2) * HD
    return pl.pallas_call(
        cut_weights_body,
        out_shape=pltpu.VMEM((n, cols), jnp.bfloat16),
        in_specs=[SMEM] + [HBM] * 3,
        out_specs=VMEM,
        scratch_shapes=[pltpu.SemaphoreType.DMA((3,))],
        compiler_params=params(2),
        cost_estimate=pl.CostEstimate(flops=0, bytes_accessed=4 * n * cols, transcendentals=0),
        name="cut_weights",
    )(index, *weights)


def gather_body(n, order, *refs):
    pieces, out, sems = refs[:n], refs[-2], refs[-1]
    rows = pieces[0].shape[0]
    copies = []
    for i, piece in enumerate(pieces):
        at = pl.ds(pl.multiple_of(order[i] * rows, 16), rows)
        copies.append(pltpu.make_async_copy(piece, out.at[at, :], sems.at[i]))
    for copy in copies:
        copy.start()
    for copy in copies:
        copy.wait()


def gather(order, pieces, deps):
    rows, cols = pieces[0].shape
    return pl.pallas_call(
        functools.partial(gather_body, len(pieces)),
        out_shape=pltpu.VMEM((rows * len(pieces), cols), jnp.bfloat16),
        in_specs=[SMEM] + [ANY] * (len(pieces) + len(deps)),
        out_specs=VMEM,
        scratch_shapes=[pltpu.SemaphoreType.DMA((len(pieces),))],
        compiler_params=params(6),
        cost_estimate=pl.CostEstimate(
            flops=0, bytes_accessed=4 * rows * cols * len(pieces), transcendentals=0
        ),
        name="gather",
    )(order, *pieces, *deps)


def cut_body(row, source, out, sem):
    copy = pltpu.make_async_copy(source.at[pl.ds(row, out.shape[0]), :], out, sem)
    copy.start()
    copy.wait()


def cut(source, block, count):
    return pl.pallas_call(
        functools.partial(cut_body, block * BLOCK),
        out_shape=pltpu.VMEM((count * BLOCK, source.shape[1]), source.dtype),
        in_specs=[HBM],
        out_specs=VMEM,
        scratch_shapes=[pltpu.SemaphoreType.DMA],
        compiler_params=params(2),
        cost_estimate=pl.CostEstimate(
            flops=0, bytes_accessed=2 * count * BLOCK * source.shape[1], transcendentals=0
        ),
        name="cut",
    )(source)


def place_body(items, sides, *refs):
    out, sems = refs[-2:]
    copies = []
    for i, (first, side) in enumerate(items):
        rows, cols = refs[i].shape
        at = pl.ds(pl.multiple_of(sides[side] * HD, HD), cols)
        copies.append(
            pltpu.make_async_copy(refs[i], out.at[pl.ds(first * BLOCK, rows), at], sems.at[i])
        )
    for copy in copies:
        copy.start()
    for copy in copies:
        copy.wait()


def place(total, sides, items, shape, deps=()):
    arrays = [array for array, _, _ in items]
    rest = list(deps) if total is None else [*deps, total]
    aliases = {} if total is None else {len(arrays) + len(rest): 0}
    return pl.pallas_call(
        functools.partial(place_body, [(first, side) for _, first, side in items]),
        out_shape=jax.ShapeDtypeStruct(shape, jnp.bfloat16),
        in_specs=[SMEM] + [VMEM] * len(arrays) + [ANY] * len(deps) + ([] if total is None else [HBM]),
        out_specs=HBM,
        scratch_shapes=[pltpu.SemaphoreType.DMA((len(arrays),))],
        input_output_aliases=aliases,
        compiler_params=params(8),
        cost_estimate=pl.CostEstimate(
            flops=0, bytes_accessed=4 * sum(a.size for a in arrays), transcendentals=0
        ),
        name="place",
    )(sides, *arrays, *rest)


def chunks_of(blocks):
    n = blocks // 4
    return [(quarter * n, n) for quarter in (2, 0, 1, 3)]


def layer(tokens, q_weight, k_weight, v_weight, q_bias, v_bias):
    n_sub = lax.axis_size("sub")
    n_ctx = lax.axis_size("ctx")
    n_head = lax.axis_size("head")
    n_groups = lax.axis_size("groups")
    rows = tokens.shape[0]
    blocks = rows // BLOCK
    nq = q_weight.shape[1]
    kvl = k_weight.shape[1] // HD
    sub = lax.axis_index("sub")
    ctx = lax.axis_index("ctx")
    head = lax.axis_index("head")
    group = lax.axis_index("groups")
    shard = ctx * n_sub + sub
    runs = chunks_of(blocks)
    weights = (q_weight, k_weight, v_weight)

    paired = n_head == 2 and kvl == 2 and n_groups == 2
    if paired:
        parts = n_groups * n_ctx
        mine = (ctx * n_groups + group).astype(jnp.int32).reshape(1)
        part = cut_weights(mine, weights, parts)
        ring = [swapped(part, "head")]
        pieces = []
        for b, n in runs:
            pieces.append(swapped(cut(tokens, b, n), "head"))
        flag = (sub == head).astype(jnp.int32).reshape(1)
        shared_bias = jnp.concatenate(
            [q_bias[nq - SHARED * HD :], jnp.zeros((HD,), jnp.float32), v_bias[(kvl - 1) * HD :]]
        )[None, :]
        shared_bias = swapped(shared_bias, "head")
        for _ in range(1, n_ctx):
            ring.append(shifted(ring[-1], "ctx", 1))
        across = []
        for d in range(n_ctx):
            across.append(swapped(ring[d], "groups"))
        turn = jnp.arange(2 * n_ctx, dtype=jnp.int32)
        there = lax.rem(ctx + n_ctx - turn % n_ctx, n_ctx) * n_groups
        part_order = jnp.where(turn < n_ctx, there + group, there + 1 - group).astype(jnp.int32)
    else:
        features = lax.all_gather(tokens, "head", axis=1, tiled=True)
        half = features.shape[1] // n_sub
        flag = (sub == 0).astype(jnp.int32).reshape(1)
        tokens = features[:, :half]
        pieces = [features[b * BLOCK : (b + n) * BLOCK, half:] for b, n in runs]
    other = swapped(k_weight, "sub"), swapped(v_weight, "sub")
    other = (swapped(q_weight, "sub"),) + other
    qb = q_bias[None, :]
    kvb = jnp.concatenate([jnp.zeros_like(v_bias), v_bias])[None, :]
    positions = (shard * rows + jnp.arange(rows, dtype=jnp.int32)).astype(jnp.float32)
    cos, sin = rotary_tables(positions)

    far_steps = [s for s in (1, 2, 4, 8) if s < n_ctx]
    biases = []
    for b, n in runs:
        steps = jnp.array(list(NEAR) + [blocks] + [n_sub * blocks * s for s in far_steps], jnp.int32)
        places = shard * blocks + b + jnp.arange(n, dtype=jnp.int32)
        biases.append(jnp.where(places[:, None] >= steps[None, :], 0.0, -1e30).astype(jnp.float32).reshape(-1))
    small = [qb, kvb, cos, sin, *biases]
    if paired:
        columns = kvl * GROUP
        sides = columns * jnp.array([0, 1, 1, 2], jnp.int32) - SHARED * jnp.array([0, 1, 0, 1], jnp.int32)
        sides = sides + head.astype(jnp.int32) * columns * jnp.array([1, 1, -1, -1], jnp.int32)
        small += [sides, part_order]
    wqa, wkva, wqb, wkvb = stage(flag, weights, other, small)
    queries, sources = {}, {}
    shared_queries, shared_sources = {}, {}

    def exchanged(kv, places, table):
        held = {"own": kv}
        held["prev"] = shifted(kv, ("ctx", "sub"), 1)
        for s in far_steps:
            held["far", s] = shifted(kv, "ctx", 1) if s == 1 else shifted(held["far", s // 2], "ctx", s // 2)
        for r, b in enumerate(places):
            for name, array in held.items():
                table[name, b] = (array, r)

    def keys_values(i, deps):
        (b, n), piece = runs[i], pieces[i]
        kv = project(tokens, b * BLOCK, piece, wkva, wkvb, kvb, cos, sin, 2 * kvl * HD, kvl, deps)
        exchanged(kv, range(b, b + n), sources)
        return (kv,)

    def all_queries(i, deps):
        (b, n), piece = runs[i], pieces[i]
        tile = 2 * HD if nq % (2 * HD) == 0 else HD
        q = project(tokens, b * BLOCK, piece, wqa, wqb, qb, cos, sin, tile, tile // HD, deps)
        for r in range(n):
            queries[b + r] = (q, r)
        return (q,)

    def neighbours_head(which, deps):
        bases = [runs[i][0] * BLOCK for i in which]
        qkv, kv = project_shared(
            tokens, bases, [pieces[i] for i in which], *shared_weights, shared_bias, cos, sin, deps
        )
        exchanged(kv, [b for i in which for b in range(runs[i][0], sum(runs[i]))], shared_sources)
        r = 0
        for i in which:
            for b in range(runs[i][0], sum(runs[i])):
                shared_queries[b] = (qkv, r)
                r += 1
        return (kv,)

    def attention(i, kind, deps):
        b0, count = runs[i]
        pair = tuple(range(b0, b0 + count))
        if kind == "neighbour":
            qs, table, form = shared_queries, shared_sources, (1, SHARED, HD, SHARED)
        else:
            n_sent = kvl * GROUP - (SHARED if paired else 0)
            qs, table, form = queries, sources, (kvl, GROUP, kvl * HD, n_sent)
        arrays, plan = [], []
        for b in pair:
            slots = []
            wanted = [(d, ("own", b - d) if d <= b else ("prev", blocks + b - d)) for d in NEAR + (blocks,)]
            wanted += [(n_sub * blocks * s, (("far", s), b)) for s in far_steps]
            for d, key in wanted:
                array, r = table[key]
                at = next((k for k, a in enumerate(arrays) if a is array), None)
                if at is None:
                    at = len(arrays)
                    arrays.append(array)
                slots.append((at, r))
            plan.append(tuple(slots))
        return attend(biases[i], *qs[b0], arrays, plan, *form, deps)

    shape = (rows, n_head * nq)
    if not paired:
        deps = ()
        for i in range(len(runs)):
            deps = keys_values(i, deps)
            deps = all_queries(i, deps)
        outs = {}
        for i, (b, _) in enumerate(runs):
            outs[b] = attention(i, "own", deps)[0]
        local = jnp.concatenate([outs[b] for b in sorted(outs)], 0)
        return lax.all_gather(local, "head", axis=1, tiled=True)

    sent, received, kept, extra = {}, {}, {}, {}

    def send(i, deps):
        sent[i], kept[i] = attention(i, "own", deps)
        received[i] = swapped(sent[i], "head")
        return (kept[i],)

    def add(i, deps):
        extra[i] = attention(i, "neighbour", deps)[0]
        return (extra[i],)

    deps = (wqa,)
    deps = keys_values(0, deps)
    deps = all_queries(0, deps)
    deps = keys_values(1, deps)
    deps = all_queries(1, deps)
    gathered = gather(part_order, ring + across, deps)
    shared_other = swapped(gathered, "sub")
    shared_weights = order_halves(flag, gathered, shared_other, (gathered,))
    deps = neighbours_head((0, 1), (shared_weights[0],))
    deps = keys_values(2, deps)
    deps = send(0, deps)
    deps = keys_values(3, deps)
    deps = all_queries(2, deps)
    deps = send(1, deps)
    deps = send(2, deps)
    deps = neighbours_head((2, 3), deps)
    deps = all_queries(3, deps)
    deps = send(3, deps)
    deps = add(0, deps)
    deps = add(1, deps)
    deps = add(2, deps)
    deps = add(3, deps)
    first = lambda i: runs[i][0]
    total = place(
        None, sides,
        [(sent[i], first(i), 0) for i in range(4)] + [(kept[i], first(i), 1) for i in range(4)]
        + [(extra[i], first(i), 3) for i in range(4)],
        shape,
    )
    total = place(total, sides, [(received[i], first(i), 2) for i in (0, 1)], shape)
    total = place(total, sides, [(received[2], first(2), 2)], shape)
    return place(total, sides, [(received[3], first(3), 2)], shape)


def solution(mesh):
    return jax.shard_map(
        layer,
        mesh=mesh,
        in_specs=(
            P(("groups", "ctx", "sub"), "head"),
            P("sub", "head"),
            P("sub", "head"),
            P("sub", "head"),
            P("head"),
            P("head"),
        ),
        out_specs=P(("groups", "ctx", "sub"), None),
        check_vma=False,
    )
```

time: 188 us -> 228 us (1.21)
  Pallas kernels: 64 us -> 83 us
  waiting for transfers between devices: 86.8 us -> 99.7 us
  starting transfers between devices: 24.4 us -> 28.9 us
  other arithmetic: 2.27 us -> 5.16 us
    ppermute x12 -> x21, waiting for transfers between devices: 13.5 us -> 42.6 us  [shifted(): lax.ppermute(value, axis, [(s, (s + steps) % count) for s in range(count)])]
    pallas_call x12 -> x17, Pallas kernels: 31.8 us -> 50.7 us  [the longest x8 33.7 us: attend(): pl.pallas_call(functools.partial(attend_body, plan, len(arrays), q_row, g...]
    ppermute x11 -> x18, waiting for transfers between devices: 73.3 us -> 57.1 us  [swapped(): return lax.ppermute(value, axis, [(0, 1), (1, 0)])]
    ppermute x11 -> x18, starting transfers between devices: 11.7 us -> 17.1 us  [swapped(): return lax.ppermute(value, axis, [(0, 1), (1, 0)])]
    ppermute x12 -> x21, starting transfers between devices: 12.7 us -> 11.8 us  [shifted(): lax.ppermute(value, axis, [(s, (s + steps) % count) for s in range(count)])]
    unnamed x28 -> x24, local copies, waits for them, and re-layouts: 9.94 us -> 9.97 us
  transfers between devices with their start and end apart: 23 -> 39, of which waited for: 10 -> 14; matrix products, arithmetic and copies ran while one was open for 1% -> 2% of each run, Pallas kernels for 34% -> 35%
where the time goes in v1:
time: 228 us
  waiting for transfers between devices  99.7 us (44%)
  Pallas kernels  83 us (36%)
  starting transfers between devices  28.9 us (13%)
  local copies, waits for them, and re-layouts  10.3 us (5%)
  other arithmetic  5.16 us (2%)
    ppermute x18, waiting for transfers between devices, swapped(): return lax.ppermute(value, axis, [(0, 1), (1, 0)])  57.1 us
    ppermute x21, waiting for transfers between devices, shifted(): lax.ppermute(value, axis, [(s, (s + steps) % count) for s in range(count)])  42.6 us
    pallas_call x8, Pallas kernels, attend(): pl.pallas_call(functools.partial(attend_body, plan, len(arrays), q_row, g...  33.7 us
    pallas_call x8, Pallas kernels, project(): pl.pallas_call(functools.partial(project_body, row, tile, rot), out_shape...  24.9 us
    ppermute x18, starting transfers between devices, swapped(): return lax.ppermute(value, axis, [(0, 1), (1, 0)])  17.1 us
    ppermute x21, starting transfers between devices, shifted(): lax.ppermute(value, axis, [(s, (s + steps) % count) for s in range(count)])  11.8 us
    unnamed x24, local copies, waits for them, and re-layouts  9.97 us
    pallas_call x4, Pallas kernels, place(): pl.pallas_call(functools.partial(place_body, [(first, side) for _, first,...  7.21 us
  transfers between devices with their start and end apart: 39, of which 14 were waited for; matrix products, arithmetic and copies ran while one was open for 2% of the time, Pallas kernels for 35%

profile of v1, /device:TPU:0, one launch (start us, length us, event | category | flops | bytes accessed | tf_op | source)
XLA Modules:
  0.0 227.8 jit_solution(3784268420712051830)
XLA Ops:
  8.9 6.9 %collective-permute-done.5.refs_0_ = bf16[224,768]{1,0:T(8,128)(2,1)S(1)} collective-permute-done((bf16[224,768]{1,0:T(8,128)(2,1)S(1)}, bf16[224,768]{1,0:T(8,128)(2,1)S(1)}, u32[]{:S(2)}, u32[]{:S(2)}) %collective-permute-start.5) | collective-permute-done | bytes 344096 | tf_op jit(solution)/shard_map/ppermute | solution.py:27
  18.0 3.2 %fusion = (f32[1024,64]{1,0:T(8,128)}, f32[1024,64]{1,0:T(8,128)}, f32[1024,64]{1,0:T(8,128)}) fusion(f32[64]{0:T(128)S(1)} %multiply_exponential_fusion, f32[1024]{0:T(1024)S(1)} %add_convert_fusion), kind=kLoop, calls=%fused_computation.4 | loop fusion | flops 131072 | bytes 790784 | tf_op jit(solution)/shard_map/neg | solution.py:36
  21.2 6.4 %collective-permute-done.6.refs_1_ = bf16[224,768]{1,0:T(8,128)(2,1)} collective-permute-done((bf16[224,768]{1,0:T(8,128)(2,1)S(1)}, bf16[224,768]{1,0:T(8,128)(2,1)}, u32[]{:S(2)}, u32[]{:S(2)}) %collective-permute-start.6) | collective-permute-done | bytes 344096 | tf_op jit(solution)/shard_map/ppermute | solution.py:23
  33.3 5.0 %collective-permute-done.7.refs_2_ = bf16[224,768]{1,0:T(8,128)(2,1)} collective-permute-done((bf16[224,768]{1,0:T(8,128)(2,1)}, bf16[224,768]{1,0:T(8,128)(2,1)}, u32[]{:S(2)}, u32[]{:S(2)}) %collective-permute-start.7) | collective-permute-done | bytes 344096 | tf_op jit(solution)/shard_map/ppermute | solution.py:23
  46.6 4.5 %stage.1 = (bf16[1792,1792]{1,0:T(8,128)(2,1)S(1)}, bf16[1792,512]{1,0:T(8,128)(2,1)S(1)}, bf16[1792,1792]{1,0:T(8,128)(2,1)S(1)}, bf16[1792,512]{1,0:T(8,128)(2,1)S(1)}) custom-call(s32[1]{0:T(128)} %bitcast.flag.refs_0_, bf16[1792,1792]{1,0:T(8,128)(2,1)S(1)} %copy-done.4, bf16[1792,256]{1,0:T(8,128)(2,1)} %wk.1, bf16[1792,256]{1,0:T(8,128)(2,1)} %wv.1, ...), custom_call_target="tpu_custom_call" | custom-call | bytes 16515072 | tf_op jit(solution)/shard_map/stage/pallas_call | solution.py:78
  54.5 5.0 %shard_map.128.refs_0_.query = bf16[256,1792]{1,0:T(8,128)(2,1)S(1)} custom-call(bf16[1024,1792]{1,0:T(8,128)(2,1)S(1)} %copy-done.2, bf16[256,1792]{1,0:T(8,128)(2,1)S(1)} %collective-permute-done.14.tb.refs_0_, bf16[1792,1792]{1,0:T(8,128)(2,1)S(1)} %get-tuple-element.23.refs_0_.wa, bf16[1792,1792]{1,0:T(8,128)(2,1)S(1)} %get-tuple-element.24.wb, ...), custom_call_target="tpu_custom_call" | custom-call | flops 3288334336 | tf_op jit(solution)/shard_map/pallas_call | solution.py:117
  60.7 5.0 %shard_map.130.refs_8_.query = bf16[256,1792]{1,0:T(8,128)(2,1)S(1)} custom-call(bf16[1024,1792]{1,0:T(8,128)(2,1)S(1)} %copy-done.2, bf16[256,1792]{1,0:T(8,128)(2,1)S(1)} %collective-permute-done.13.tb.refs_1_, bf16[1792,1792]{1,0:T(8,128)(2,1)S(1)} %get-tuple-element.23.refs_0_.wa, bf16[1792,1792]{1,0:T(8,128)(2,1)S(1)} %get-tuple-element.24.wb, ...), custom_call_target="tpu_custom_call" | custom-call | flops 3288334336 | tf_op jit(solution)/shard_map/pallas_call | solution.py:117
  66.3 4.2 %collective-permute-done.12.refs_7_ = bf16[224,768]{1,0:T(8,128)(2,1)S(1)} collective-permute-done((bf16[224,768]{1,0:T(8,128)(2,1)}, bf16[224,768]{1,0:T(8,128)(2,1)S(1)}, u32[]{:S(2)}, u32[]{:S(2)}) %collective-permute-start.12) | collective-permute-done | bytes 344096 | tf_op jit(solution)/shard_map/ppermute | solution.py:27
  78.4 36.8 %collective-permute-done.16.refs_4_ = f32[1,768]{1,0:T(1,128)S(1)} collective-permute-done((f32[1,768]{1,0:T(1,128)S(1)}, f32[1,768]{1,0:T(1,128)S(1)}, u32[]{:S(2)}, u32[]{:S(2)}) %collective-permute-start.16) | collective-permute-done | bytes 3104 | tf_op jit(solution)/shard_map/ppermute | solution.py:27
  115.6 3.1 %project_shared.2 = (bf16[512,512]{1,0:T(8,128)(2,1)S(1)}, bf16[512,256]{1,0:T(8,128)(2,1)S(1)}) custom-call(bf16[1024,1792]{1,0:T(8,128)(2,1)S(1)} %copy-done.2, bf16[256,1792]{1,0:T(8,128)(2,1)S(1)} %collective-permute-done.14.tb.refs_0_, bf16[256,1792]{1,0:T(8,128)(2,1)S(1)} %collective-permute-done.13.tb.refs_1_, ...), custom_call_target="tpu_custom_call" | custom-call | flops 2818572288 | tf_op jit(solution)/shard_map/project_shared/pallas_call | solution.py:256
  118.8 7.3 %collective-permute-done.25.refs_4_ = bf16[256,512]{1,0:T(8,128)(2,1)S(1)} collective-permute-done((bf16[256,512]{1,0:T(8,128)(2,1)S(1)}, bf16[256,512]{1,0:T(8,128)(2,1)S(1)}, u32[]{:S(2)}, u32[]{:S(2)}) %collective-permute-start.25) | collective-permute-done | bytes 262176 | tf_op jit(solution)/shard_map/ppermute | solution.py:23
  127.8 4.0 %collective-permute-done.19.refs_5_ = bf16[256,512]{1,0:T(8,128)(2,1)S(1)} collective-permute-done((bf16[256,512]{1,0:T(8,128)(2,1)S(1)}, bf16[256,512]{1,0:T(8,128)(2,1)S(1)}, u32[]{:S(2)}, u32[]{:S(2)}) %collective-permute-start.19) | collective-permute-done | bytes 262176 | tf_op jit(solution)/shard_map/ppermute | solution.py:23
  131.8 6.1 %attend.8 = (bf16[256,1280]{1,0:T(8,128)(2,1)S(1)}, bf16[256,512]{1,0:T(8,128)(2,1)S(1)}) custom-call(f32[14]{0:T(128)S(1)} %select_n.43.refs_10_.bias, bf16[256,1792]{1,0:T(8,128)(2,1)S(1)} %shard_map.128.refs_0_.query, bf16[256,512]{1,0:T(8,128)(2,1)S(1)} %shard_map.127.refs_0_.refs_1_, bf16[256,512]{1,0:T(8,128)(2,1)S(1)} %shard_map.131.refs_1_.refs_6_.refs_0_.refs_2_, ...), custom_call_target="tpu_custom_call" | custom-call | flops 1644167168 | tf_op jit(solution)/shard_map/attend/pallas_call | solution.py:174
  144.2 5.0 %shard_map.133.refs_6_.query = bf16[256,1792]{1,0:T(8,128)(2,1)S(1)} custom-call(bf16[1024,1792]{1,0:T(8,128)(2,1)S(1)} %copy-done.2, bf16[256,1792]{1,0:T(8,128)(2,1)S(1)} %collective-permute-done.4.tb.refs_0_, bf16[1792,1792]{1,0:T(8,128)(2,1)S(1)} %get-tuple-element.23.refs_0_.wa, bf16[1792,1792]{1,0:T(8,128)(2,1)S(1)} %get-tuple-element.24.wb, ...), custom_call_target="tpu_custom_call" | custom-call | flops 3288334336 | tf_op jit(solution)/shard_map/pallas_call | solution.py:117
  149.3 6.4 %collective-permute-done.20.refs_1_.refs_2_.refs_3_ = bf16[256,512]{1,0:T(8,128)(2,1)S(1)} collective-permute-done((bf16[256,512]{1,0:T(8,128)(2,1)S(1)}, bf16[256,512]{1,0:T(8,128)(2,1)S(1)}, u32[]{:S(2)}, u32[]{:S(2)}) %collective-permute-start.20) | collective-permute-done | bytes 262176 | tf_op jit(solution)/shard_map/ppermute | solution.py:23
  155.7 6.1 %attend.9 = (bf16[256,1280]{1,0:T(8,128)(2,1)S(1)}, bf16[256,512]{1,0:T(8,128)(2,1)S(1)}) custom-call(f32[14]{0:T(128)S(1)} %select_n.45.refs_11_.bias, bf16[256,1792]{1,0:T(8,128)(2,1)S(1)} %shard_map.130.refs_8_.query, bf16[256,512]{1,0:T(8,128)(2,1)S(1)} %shard_map.129.refs_0_.refs_2_.refs_1_, ...), custom_call_target="tpu_custom_call" | custom-call | flops 1644167168 | tf_op jit(solution)/shard_map/attend/pallas_call | solution.py:174
  163.1 6.1 %attend.10 = (bf16[256,1280]{1,0:T(8,128)(2,1)S(1)}, bf16[256,512]{1,0:T(8,128)(2,1)S(1)}) custom-call(f32[14]{0:T(128)S(1)} %select_n.47.refs_12_.bias, bf16[256,1792]{1,0:T(8,128)(2,1)S(1)} %shard_map.133.refs_6_.query, bf16[256,512]{1,0:T(8,128)(2,1)S(1)} %shard_map.131.refs_1_.refs_6_.refs_0_.refs_2_, ...), custom_call_target="tpu_custom_call" | custom-call | flops 1644167168 | tf_op jit(solution)/shard_map/attend/pallas_call | solution.py:174
  169.2 3.2 %project_shared.3 = (bf16[512,512]{1,0:T(8,128)(2,1)S(1)}, bf16[512,256]{1,0:T(8,128)(2,1)S(1)}) custom-call(bf16[1024,1792]{1,0:T(8,128)(2,1)S(1)} %copy-done.2, bf16[256,1792]{1,0:T(8,128)(2,1)S(1)} %collective-permute-done.4.tb.refs_0_, bf16[256,1792]{1,0:T(8,128)(2,1)S(1)} %collective-permute-done.tb.refs_1_, ...), custom_call_target="tpu_custom_call" | custom-call | flops 2818572288 | tf_op jit(solution)/shard_map/project_shared/pallas_call | solution.py:256
  172.3 4.0 %collective-permute-start.36 = (bf16[512,256]{1,0:T(8,128)(2,1)S(1)}, bf16[512,256]{1,0:T(8,128)(2,1)S(1)}, u32[]{:S(2)}, u32[]{:S(2)}) collective-permute-start(bf16[512,256]{1,0:T(8,128)(2,1)S(1)} %get-tuple-element.33.refs_0_.refs_1_), channel_id=1, source_target_pairs={{0,1},{1,4},{4,5},{5,8},{8,9},{9,12},{12,13},{13,0},{2,3},{3,6},{6... | collective-permute-start | bytes 786440 | tf_op jit(solution)/shard_map/ppermute | solution.py:23
  176.3 5.0 %shard_map.134.query.refs_6_ = bf16[256,1792]{1,0:T(8,128)(2,1)S(1)} custom-call(bf16[1024,1792]{1,0:T(8,128)(2,1)S(1)} %copy-done.2, bf16[256,1792]{1,0:T(8,128)(2,1)S(1)} %collective-permute-done.tb.refs_1_, bf16[1792,1792]{1,0:T(8,128)(2,1)S(1)} %get-tuple-element.23.refs_0_.wa, bf16[1792,1792]{1,0:T(8,128)(2,1)S(1)} %get-tuple-element.24.wb, ...), custom_call_target="tpu_custom_call" | custom-call | flops 3288334336 | tf_op jit(solution)/shard_map/pallas_call | solution.py:117
  182.5 6.1 %attend.11 = (bf16[256,1280]{1,0:T(8,128)(2,1)S(1)}, bf16[256,512]{1,0:T(8,128)(2,1)S(1)}) custom-call(f32[14]{0:T(128)S(1)} %select_n.41.refs_13_.bias, bf16[256,1792]{1,0:T(8,128)(2,1)S(1)} %shard_map.134.query.refs_6_, bf16[256,512]{1,0:T(8,128)(2,1)S(1)} %shard_map.132.refs_0_, bf16[256,512]{1,0:T(8,128)(2,1)S(1)} %shard_map.127.refs_0_.refs_1_, ...), custom_call_target="tpu_custom_call" | custom-call | flops 1644167168 | tf_op jit(solution)/shard_map/attend/pallas_call | solution.py:174
  190.9 9.0 %collective-permute-done.37.refs_3_ = bf16[512,256]{1,0:T(8,128)(2,1)S(1)} collective-permute-done((bf16[512,256]{1,0:T(8,128)(2,1)S(1)}, bf16[512,256]{1,0:T(8,128)(2,1)S(1)}, u32[]{:S(2)}, u32[]{:S(2)}) %collective-permute-start.37) | collective-permute-done | bytes 262176 | tf_op jit(solution)/shard_map/ppermute | solution.py:23
  204.6 3.6 %collective-permute-done.38.refs_4_ = bf16[512,256]{1,0:T(8,128)(2,1)S(1)} collective-permute-done((bf16[512,256]{1,0:T(8,128)(2,1)S(1)}, bf16[512,256]{1,0:T(8,128)(2,1)S(1)}, u32[]{:S(2)}, u32[]{:S(2)}) %collective-permute-start.38) | collective-permute-done | bytes 262176 | tf_op jit(solution)/shard_map/ppermute | solution.py:23
  218.8 7.4 %collective-permute-done.29.refs_0_ = bf16[256,1280]{1,0:T(8,128)(2,1)S(1)} collective-permute-done((bf16[256,1280]{1,0:T(8,128)(2,1)S(1)}, bf16[256,1280]{1,0:T(8,128)(2,1)S(1)}, u32[]{:S(2)}, u32[]{:S(2)}) %collective-permute-start.29) | collective-permute-done | bytes 655392 | tf_op jit(solution)/shard_map/ppermute | solution.py:27
  (128 shorter events, 67.6 us)
Async XLA Ops:
  0.0 41.9 %collective-permute-start.1 = (bf16[1792,1792]{1,0:T(8,128)(2,1)}, bf16[1792,1792]{1,0:T(8,128)(2,1)}, u32[]{:S(2)}, u32[]{:S(2)}) collective-permute-start(bf16[1792,1792]{1,0:T(8,128)(2,1)} %wq.1), channel_id=1, source_target_pairs={{0,1},{1,0},{2,3},{3,2},{4,5},{5,4},{6,7},{7,6},{8,9},{9,8},{10,11... | collective-permute-start | bytes 19267592 | tf_op jit(solution)/shard_map/ppermute | solution.py:27
  7.0 23.8 %collective-permute-start.2 = (bf16[1792,256]{1,0:T(8,128)(2,1)}, bf16[1792,256]{1,0:T(8,128)(2,1)S(1)}, u32[]{:S(2)}, u32[]{:S(2)}) collective-permute-start(bf16[1792,256]{1,0:T(8,128)(2,1)} %wk.1), channel_id=1, source_target_pairs={{0,1},{1,0},{2,3},{3,2},{4,5},{5,4},{6,7},{7,6},{8,9},{9,8},{10,11... | collective-permute-start | bytes 2752520 | tf_op jit(solution)/shard_map/ppermute | solution.py:27
  7.2 33.3 %collective-permute-start.3 = (bf16[1792,256]{1,0:T(8,128)(2,1)}, bf16[1792,256]{1,0:T(8,128)(2,1)}, u32[]{:S(2)}, u32[]{:S(2)}) collective-permute-start(bf16[1792,256]{1,0:T(8,128)(2,1)} %wv.1), channel_id=1, source_target_pairs={{0,1},{1,0},{2,3},{3,2},{4,5},{5,4},{6,7},{7,6},{8,9},{9,8},{10,11... | collective-permute-start | bytes 2752520 | tf_op jit(solution)/shard_map/ppermute | solution.py:27
  8.7 42.5 %collective-permute-start.14 = (bf16[256,1792]{1,0:T(8,128)(2,1)}, bf16[256,1792]{1,0:T(8,128)(2,1)S(1)}, u32[]{:S(2)}, u32[]{:S(2)}) collective-permute-start(bf16[256,1792]{1,0:T(8,128)(2,1)} %cut.7), channel_id=1, source_target_pairs={{0,2},{2,0},{1,3},{3,1},{4,6},{6,4},{5,7},{7,5},{8,10},{10,8},{9,1... | collective-permute-start | bytes 2752520 | tf_op jit(solution)/shard_map/ppermute | solution.py:27
  31.7 27.8 %collective-permute-start.13 = (bf16[256,1792]{1,0:T(8,128)(2,1)}, bf16[256,1792]{1,0:T(8,128)(2,1)S(1)}, u32[]{:S(2)}, u32[]{:S(2)}) collective-permute-start(bf16[256,1792]{1,0:T(8,128)(2,1)} %cut.6), channel_id=1, source_target_pairs={{0,2},{2,0},{1,3},{3,1},{4,6},{6,4},{5,7},{7,5},{8,10},{10,8},{9,1... | collective-permute-start | bytes 2752520 | tf_op jit(solution)/shard_map/ppermute | solution.py:27
  40.5 25.3 %collective-permute-start.9 = (bf16[224,768]{1,0:T(8,128)(2,1)S(1)}, bf16[224,768]{1,0:T(8,128)(2,1)S(1)}, u32[]{:S(2)}, u32[]{:S(2)}) collective-permute-start(bf16[224,768]{1,0:T(8,128)(2,1)S(1)} %collective-permute-done.5.refs_0_), channel_id=1, source_target_pairs={{0,16},{16,0},{1,17},{17,1},{2,18},{18,2},{3,19},{19,3},{4,20},{20... | collective-permute-start | bytes 1032200 | tf_op jit(solution)/shard_map/ppermute | solution.py:27
  41.9 23.9 %collective-permute-start.10 = (bf16[224,768]{1,0:T(8,128)(2,1)}, bf16[224,768]{1,0:T(8,128)(2,1)S(1)}, u32[]{:S(2)}, u32[]{:S(2)}) collective-permute-start(bf16[224,768]{1,0:T(8,128)(2,1)} %collective-permute-done.6.refs_1_), channel_id=1, source_target_pairs={{0,16},{16,0},{1,17},{17,1},{2,18},{18,2},{3,19},{19,3},{4,20},{20... | collective-permute-start | bytes 1032200 | tf_op jit(solution)/shard_map/ppermute | solution.py:27
  72.7 46.1 %collective-permute-start.4 = (bf16[256,1792]{1,0:T(8,128)(2,1)S(1)}, bf16[256,1792]{1,0:T(8,128)(2,1)S(1)}, u32[]{:S(2)}, u32[]{:S(2)}) collective-permute-start(bf16[256,1792]{1,0:T(8,128)(2,1)S(1)} %cut.5), channel_id=1, source_target_pairs={{0,2},{2,0},{1,3},{3,1},{4,6},{6,4},{5,7},{7,5},{8,10},{10,8},{9,1... | collective-permute-start | bytes 2752520 | tf_op jit(solution)/shard_map/ppermute | solution.py:27
  74.0 63.9 %collective-permute-start = (bf16[256,1792]{1,0:T(8,128)(2,1)S(1)}, bf16[256,1792]{1,0:T(8,128)(2,1)S(1)}, u32[]{:S(2)}, u32[]{:S(2)}) collective-permute-start(bf16[256,1792]{1,0:T(8,128)(2,1)S(1)} %cut.4), channel_id=1, source_target_pairs={{0,2},{2,0},{1,3},{3,1},{4,6},{6,4},{5,7},{7,5},{8,10},{10,8},{9,1... | collective-permute-start | bytes 2752520 | tf_op jit(solution)/shard_map/ppermute | solution.py:27
  75.1 40.2 %collective-permute-start.18 = (bf16[256,512]{1,0:T(8,128)(2,1)S(1)}, bf16[256,512]{1,0:T(8,128)(2,1)S(1)}, u32[]{:S(2)}, u32[]{:S(2)}) collective-permute-start(bf16[256,512]{1,0:T(8,128)(2,1)S(1)} %shard_map.127.refs_0_.refs_1_), channel_id=1, source_target_pairs={{0,4},{4,8},{8,12},{12,0},{1,5},{5,9},{9,13},{13,1},{2,6},{6,10},{... | collective-permute-start | bytes 786440 | tf_op jit(solution)/shard_map/ppermute | solution.py:23
  75.1 40.1 %collective-permute-start.16 = (f32[1,768]{1,0:T(1,128)S(1)}, f32[1,768]{1,0:T(1,128)S(1)}, u32[]{:S(2)}, u32[]{:S(2)}) collective-permute-start(f32[1,768]{1,0:T(1,128)S(1)} %broadcast_in_dim.42), channel_id=1, source_target_pairs={{0,2},{2,0},{1,3},{3,1},{4,6},{6,4},{5,7},{7,5},{8,10},{10,8},{9,1... | collective-permute-start | bytes 9224 | tf_op jit(solution)/shard_map/ppermute | solution.py:27
  77.5 49.9 %collective-permute-start.17 = (bf16[256,512]{1,0:T(8,128)(2,1)S(1)}, bf16[256,512]{1,0:T(8,128)(2,1)S(1)}, u32[]{:S(2)}, u32[]{:S(2)}) collective-permute-start(bf16[256,512]{1,0:T(8,128)(2,1)S(1)} %shard_map.127.refs_0_.refs_1_), channel_id=1, source_target_pairs={{0,1},{1,4},{4,5},{5,8},{8,9},{9,12},{12,13},{13,0},{2,3},{3,6},{6... | collective-permute-start | bytes 786440 | tf_op jit(solution)/shard_map/ppermute | solution.py:23
  118.8 20.4 %collective-permute-start.24 = (bf16[256,512]{1,0:T(8,128)(2,1)S(1)}, bf16[256,512]{1,0:T(8,128)(2,1)S(1)}, u32[]{:S(2)}, u32[]{:S(2)}) collective-permute-start(bf16[256,512]{1,0:T(8,128)(2,1)S(1)} %shard_map.129.refs_0_.refs_2_.refs_1_), channel_id=1, source_target_pairs={{0,1},{1,4},{4,5},{5,8},{8,9},{9,12},{12,13},{13,0},{2,3},{3,6},{6... | collective-permute-start | bytes 786440 | tf_op jit(solution)/shard_map/ppermute | solution.py:23
  131.8 29.9 %collective-permute-start.21 = (bf16[256,512]{1,0:T(8,128)(2,1)S(1)}, bf16[256,512]{1,0:T(8,128)(2,1)S(1)}, u32[]{:S(2)}, u32[]{:S(2)}) collective-permute-start(bf16[256,512]{1,0:T(8,128)(2,1)S(1)} %shard_map.131.refs_1_.refs_6_.refs_0_.refs_2_), channel_id=1, source_target_pairs={{0,1},{1,4},{4,5},{5,8},{8,9},{9,12},{12,13},{13,0},{2,3},{3,6},{6... | collective-permute-start | bytes 786440 | tf_op jit(solution)/shard_map/ppermute | solution.py:23
  139.2 23.7 %collective-permute-start.27 = (bf16[256,512]{1,0:T(8,128)(2,1)S(1)}, bf16[256,512]{1,0:T(8,128)(2,1)S(1)}, u32[]{:S(2)}, u32[]{:S(2)}) collective-permute-start(bf16[256,512]{1,0:T(8,128)(2,1)S(1)} %shard_map.132.refs_0_), channel_id=1, source_target_pairs={{0,4},{4,8},{8,12},{12,0},{1,5},{5,9},{9,13},{13,1},{2,6},{6,10},{... | collective-permute-start | bytes 786440 | tf_op jit(solution)/shard_map/ppermute | solution.py:23
  139.9 23.0 %collective-permute-start.34 = (bf16[512,256]{1,0:T(8,128)(2,1)S(1)}, bf16[512,256]{1,0:T(8,128)(2,1)S(1)}, u32[]{:S(2)}, u32[]{:S(2)}) collective-permute-start(bf16[512,256]{1,0:T(8,128)(2,1)S(1)} %get-tuple-element.29.refs_0_.refs_1_), channel_id=1, source_target_pairs={{0,4},{4,8},{8,12},{12,0},{1,5},{5,9},{9,13},{13,1},{2,6},{6,10},{... | collective-permute-start | bytes 786440 | tf_op jit(solution)/shard_map/ppermute | solution.py:23
  143.1 20.0 %collective-permute-start.23 = (bf16[256,512]{1,0:T(8,128)(2,1)S(1)}, bf16[256,512]{1,0:T(8,128)(2,1)S(1)}, u32[]{:S(2)}, u32[]{:S(2)}) collective-permute-start(bf16[256,512]{1,0:T(8,128)(2,1)S(1)} %collective-permute-done.22.refs_4_), channel_id=1, source_target_pairs={{0,4},{4,8},{8,12},{12,0},{1,5},{5,9},{9,13},{13,1},{2,6},{6,10},{... | collective-permute-start | bytes 786440 | tf_op jit(solution)/shard_map/ppermute | solution.py:23
  155.7 32.9 %collective-permute-start.33 = (bf16[512,256]{1,0:T(8,128)(2,1)S(1)}, bf16[512,256]{1,0:T(8,128)(2,1)S(1)}, u32[]{:S(2)}, u32[]{:S(2)}) collective-permute-start(bf16[512,256]{1,0:T(8,128)(2,1)S(1)} %get-tuple-element.29.refs_0_.refs_1_), channel_id=1, source_target_pairs={{0,1},{1,4},{4,5},{5,8},{8,9},{9,12},{12,13},{13,0},{2,3},{3,6},{6... | collective-permute-start | bytes 786440 | tf_op jit(solution)/shard_map/ppermute | solution.py:23
  161.7 54.0 %collective-permute-start.31 = (bf16[256,1280]{1,0:T(8,128)(2,1)S(1)}, bf16[256,1280]{1,0:T(8,128)(2,1)S(1)}, u32[]{:S(2)}, u32[]{:S(2)}) collective-permute-start(bf16[256,1280]{1,0:T(8,128)(2,1)S(1)} %get-tuple-element.36.refs_0_), channel_id=1, source_target_pairs={{0,2},{2,0},{1,3},{3,1},{4,6},{6,4},{5,7},{7,5},{8,10},{10,8},{9,1... | collective-permute-start | bytes 1966088 | tf_op jit(solution)/shard_map/ppermute | solution.py:27
  162.9 18.5 %collective-permute-start.28 = (bf16[256,512]{1,0:T(8,128)(2,1)S(1)}, bf16[256,512]{1,0:T(8,128)(2,1)S(1)}, u32[]{:S(2)}, u32[]{:S(2)}) collective-permute-start(bf16[256,512]{1,0:T(8,128)(2,1)S(1)} %collective-permute-done.27.refs_4_), channel_id=1, source_target_pairs={{0,4},{4,8},{8,12},{12,0},{1,5},{5,9},{9,13},{13,1},{2,6},{6,10},{... | collective-permute-start | bytes 786440 | tf_op jit(solution)/shard_map/ppermute | solution.py:23
  162.9 26.8 %collective-permute-start.35 = (bf16[512,256]{1,0:T(8,128)(2,1)S(1)}, bf16[512,256]{1,0:T(8,128)(2,1)S(1)}, u32[]{:S(2)}, u32[]{:S(2)}) collective-permute-start(bf16[512,256]{1,0:T(8,128)(2,1)S(1)} %collective-permute-done.34.refs_3_), channel_id=1, source_target_pairs={{0,4},{4,8},{8,12},{12,0},{1,5},{5,9},{9,13},{13,1},{2,6},{6,10},{... | collective-permute-start | bytes 786440 | tf_op jit(solution)/shard_map/ppermute | solution.py:23
  181.4 34.4 %collective-permute-start.32 = (bf16[256,1280]{1,0:T(8,128)(2,1)S(1)}, bf16[256,1280]{1,0:T(8,128)(2,1)S(1)}, u32[]{:S(2)}, u32[]{:S(2)}) collective-permute-start(bf16[256,1280]{1,0:T(8,128)(2,1)S(1)} %get-tuple-element.37.refs_1_), channel_id=1, source_target_pairs={{0,2},{2,0},{1,3},{3,1},{4,6},{6,4},{5,7},{7,5},{8,10},{10,8},{9,1... | collective-permute-start | bytes 1966088 | tf_op jit(solution)/shard_map/ppermute | solution.py:27
  188.6 28.8 %collective-permute-start.30 = (bf16[256,1280]{1,0:T(8,128)(2,1)S(1)}, bf16[256,1280]{1,0:T(8,128)(2,1)S(1)}, u32[]{:S(2)}, u32[]{:S(2)}) collective-permute-start(bf16[256,1280]{1,0:T(8,128)(2,1)S(1)} %get-tuple-element.35.refs_2_), channel_id=1, source_target_pairs={{0,2},{2,0},{1,3},{3,1},{4,6},{6,4},{5,7},{7,5},{8,10},{10,8},{9,1... | collective-permute-start | bytes 1966088 | tf_op jit(solution)/shard_map/ppermute | solution.py:27
  189.6 36.5 %collective-permute-start.29 = (bf16[256,1280]{1,0:T(8,128)(2,1)S(1)}, bf16[256,1280]{1,0:T(8,128)(2,1)S(1)}, u32[]{:S(2)}, u32[]{:S(2)}) collective-permute-start(bf16[256,1280]{1,0:T(8,128)(2,1)S(1)} %get-tuple-element.34.refs_3_), channel_id=1, source_target_pairs={{0,2},{2,0},{1,3},{3,1},{4,6},{6,4},{5,7},{7,5},{8,10},{10,8},{9,1... | collective-permute-start | bytes 1966088 | tf_op jit(solution)/shard_map/ppermute | solution.py:27
  (27 other events, 392.2 us)

commit v2 on v1

--- a/solution.py
+++ b/solution.py
@@ -379,7 +379,7 @@
         out_specs=HBM,
         scratch_shapes=[pltpu.SemaphoreType.DMA((len(arrays),))],
         input_output_aliases=aliases,
-        compiler_params=params(8),
+        compiler_params=params(3),
         cost_estimate=pl.CostEstimate(
             flops=0, bytes_accessed=4 * sum(a.size for a in arrays), transcendentals=0
         ),
@@ -553,26 +553,28 @@
     deps = neighbours_head((0, 1), (shared_weights[0],))
     deps = keys_values(2, deps)
     deps = send(0, deps)
+    deps = all_queries(2, deps)
     deps = keys_values(3, deps)
-    deps = all_queries(2, deps)
+    deps = neighbours_head((2, 3), deps)
     deps = send(1, deps)
     deps = send(2, deps)
-    deps = neighbours_head((2, 3), deps)
     deps = all_queries(3, deps)
     deps = send(3, deps)
     deps = add(0, deps)
     deps = add(1, deps)
-    deps = add(2, deps)
-    deps = add(3, deps)
     first = lambda i: runs[i][0]
     total = place(
         None, sides,
         [(sent[i], first(i), 0) for i in range(4)] + [(kept[i], first(i), 1) for i in range(4)]
-        + [(extra[i], first(i), 3) for i in range(4)],
-        shape,
+        + [(extra[i], first(i), 3) for i in (0, 1)],
+        shape, deps,
     )
-    total = place(total, sides, [(received[i], first(i), 2) for i in (0, 1)], shape)
-    total = place(total, sides, [(received[2], first(2), 2)], shape)
+    deps = add(2, deps)
+    deps = add(3, deps)
+    total = place(
+        total, sides,
+        [(extra[i], first(i), 3) for i in (2, 3)] + [(received[i], first(i), 2) for i in (0, 1, 2)], shape,
+    )
     return place(total, sides, [(received[3], first(3), 2)], shape)
 
 

time: 228 us -> 239 us (1.048)
  the two profiles are of different devices: /device:TPU:0 before, /device:TPU:1 now
where the time goes in v2:
time: 239 us; the launch traced here: 238 us
  waiting for transfers between devices  110 us (46%)
  Pallas kernels  81.1 us (34%)
  starting transfers between devices  31.1 us (13%)
  local copies, waits for them, and re-layouts  10.3 us (4%)
  other arithmetic  5.16 us (2%)
    ppermute x18, waiting for transfers between devices, swapped(): return lax.ppermute(value, axis, [(0, 1), (1, 0)])  71.8 us
    ppermute x21, waiting for transfers between devices, shifted(): lax.ppermute(value, axis, [(s, (s + steps) % count) for s in range(count)])  38.2 us
    pallas_call x8, Pallas kernels, attend(): pl.pallas_call(functools.partial(attend_body, plan, len(arrays), q_row, g...  33.7 us
    pallas_call x8, Pallas kernels, project(): pl.pallas_call(functools.partial(project_body, row, tile, rot), out_shape...  24.9 us
    ppermute x18, starting transfers between devices, swapped(): return lax.ppermute(value, axis, [(0, 1), (1, 0)])  16.6 us
    ppermute x21, starting transfers between devices, shifted(): lax.ppermute(value, axis, [(s, (s + steps) % count) for s in range(count)])  14.5 us
    unnamed x24, local copies, waits for them, and re-layouts  9.97 us
    pallas_call x2, Pallas kernels, project_shared(): pl.pallas_call(functools.partial(project_shared_body, bases), out_shape=(...  6.29 us
  transfers between devices with their start and end apart: 39, of which 15 were waited for; matrix products, arithmetic and copies ran while one was open for 2% of the time, Pallas kernels for 33%

profile of v2, /device:TPU:1, one launch (start us, length us, event | category | flops | bytes accessed | tf_op | source)
XLA Modules:
  0.0 238.4 jit_solution(17423361364492811276)
XLA Ops:
  8.6 6.5 %collective-permute-done.7.refs_0_ = bf16[224,768]{1,0:T(8,128)(2,1)S(1)} collective-permute-done((bf16[224,768]{1,0:T(8,128)(2,1)S(1)}, bf16[224,768]{1,0:T(8,128)(2,1)S(1)}, u32[]{:S(2)}, u32[]{:S(2)}) %collective-permute-start.7) | collective-permute-done | bytes 344096 | tf_op jit(solution)/shard_map/ppermute | solution.py:27
  16.4 3.2 %fusion = (f32[1024,64]{1,0:T(8,128)}, f32[1024,64]{1,0:T(8,128)}, f32[1024,64]{1,0:T(8,128)}) fusion(f32[64]{0:T(128)S(1)} %multiply_exponential_fusion, f32[1024]{0:T(1024)S(1)} %add_convert_fusion), kind=kLoop, calls=%fused_computation.4 | loop fusion | flops 131072 | bytes 790784 | tf_op jit(solution)/shard_map/neg | solution.py:36
  19.6 6.1 %collective-permute-done.8.refs_1_ = bf16[224,768]{1,0:T(8,128)(2,1)} collective-permute-done((bf16[224,768]{1,0:T(8,128)(2,1)S(1)}, bf16[224,768]{1,0:T(8,128)(2,1)}, u32[]{:S(2)}, u32[]{:S(2)}) %collective-permute-start.8) | collective-permute-done | bytes 344096 | tf_op jit(solution)/shard_map/ppermute | solution.py:23
  30.9 4.6 %collective-permute-done.9.refs_2_ = bf16[224,768]{1,0:T(8,128)(2,1)} collective-permute-done((bf16[224,768]{1,0:T(8,128)(2,1)}, bf16[224,768]{1,0:T(8,128)(2,1)}, u32[]{:S(2)}, u32[]{:S(2)}) %collective-permute-start.9) | collective-permute-done | bytes 344096 | tf_op jit(solution)/shard_map/ppermute | solution.py:23
  43.3 3.9 %stage.1 = (bf16[1792,1792]{1,0:T(8,128)(2,1)S(1)}, bf16[1792,512]{1,0:T(8,128)(2,1)S(1)}, bf16[1792,1792]{1,0:T(8,128)(2,1)S(1)}, bf16[1792,512]{1,0:T(8,128)(2,1)S(1)}) custom-call(s32[1]{0:T(128)} %bitcast.flag.refs_0_, bf16[1792,1792]{1,0:T(8,128)(2,1)S(1)} %copy-done.4, bf16[1792,256]{1,0:T(8,128)(2,1)} %wk.1, bf16[1792,256]{1,0:T(8,128)(2,1)} %wv.1, ...), custom_call_target="tpu_custom_call" | custom-call | bytes 16515072 | tf_op jit(solution)/shard_map/stage/pallas_call | solution.py:78
  49.9 5.0 %shard_map.128.refs_0_.query = bf16[256,1792]{1,0:T(8,128)(2,1)S(1)} custom-call(bf16[1024,1792]{1,0:T(8,128)(2,1)S(1)} %copy-done.2, bf16[256,1792]{1,0:T(8,128)(2,1)S(1)} %collective-permute-done.5.tb.refs_0_, bf16[1792,1792]{1,0:T(8,128)(2,1)S(1)} %get-tuple-element.23.refs_0_.wa, bf16[1792,1792]{1,0:T(8,128)(2,1)S(1)} %get-tuple-element.24.wb, ...), custom_call_target="tpu_custom_call" | custom-call | flops 3288334336 | tf_op jit(solution)/shard_map/pallas_call | solution.py:117
  56.2 5.0 %shard_map.130.refs_8_.query = bf16[256,1792]{1,0:T(8,128)(2,1)S(1)} custom-call(bf16[1024,1792]{1,0:T(8,128)(2,1)S(1)} %copy-done.2, bf16[256,1792]{1,0:T(8,128)(2,1)S(1)} %collective-permute-done.6.tb.refs_1_, bf16[1792,1792]{1,0:T(8,128)(2,1)S(1)} %get-tuple-element.23.refs_0_.wa, bf16[1792,1792]{1,0:T(8,128)(2,1)S(1)} %get-tuple-element.24.wb, ...), custom_call_target="tpu_custom_call" | custom-call | flops 3288334336 | tf_op jit(solution)/shard_map/pallas_call | solution.py:117
  61.2 5.6 %collective-permute-done.14.refs_7_ = bf16[224,768]{1,0:T(8,128)(2,1)S(1)} collective-permute-done((bf16[224,768]{1,0:T(8,128)(2,1)}, bf16[224,768]{1,0:T(8,128)(2,1)S(1)}, u32[]{:S(2)}, u32[]{:S(2)}) %collective-permute-start.14) | collective-permute-done | bytes 344096 | tf_op jit(solution)/shard_map/ppermute | solution.py:27
  68.8 3.7 %collective-permute-start.15 = (bf16[1792,768]{1,0:T(8,128)(2,1)S(1)}, bf16[1792,768]{1,0:T(8,128)(2,1)S(1)}, u32[]{:S(2)}, u32[]{:S(2)}) collective-permute-start(bf16[1792,768]{1,0:T(8,128)(2,1)S(1)} %gather.1.refs_1_.refs_3_), channel_id=1, source_target_pairs={{0,1},{1,0},{2,3},{3,2},{4,5},{5,4},{6,7},{7,6},{8,9},{9,8},{10,11... | collective-permute-start | bytes 8257544 | tf_op jit(solution)/shard_map/ppermute | solution.py:27
  77.9 36.5 %collective-permute-done.16.refs_4_ = f32[1,768]{1,0:T(1,128)S(1)} collective-permute-done((f32[1,768]{1,0:T(1,128)S(1)}, f32[1,768]{1,0:T(1,128)S(1)}, u32[]{:S(2)}, u32[]{:S(2)}) %collective-permute-start.16) | collective-permute-done | bytes 3104 | tf_op jit(solution)/shard_map/ppermute | solution.py:27
  114.4 3.1 %project_shared.2 = (bf16[512,512]{1,0:T(8,128)(2,1)S(1)}, bf16[512,256]{1,0:T(8,128)(2,1)S(1)}) custom-call(bf16[1024,1792]{1,0:T(8,128)(2,1)S(1)} %copy-done.2, bf16[256,1792]{1,0:T(8,128)(2,1)S(1)} %collective-permute-done.5.tb.refs_0_, bf16[256,1792]{1,0:T(8,128)(2,1)S(1)} %collective-permute-done.6.tb.refs_1_, ...), custom_call_target="tpu_custom_call" | custom-call | flops 2818572288 | tf_op jit(solution)/shard_map/project_shared/pallas_call | solution.py:256
  117.5 5.2 %collective-permute-start.24 = (bf16[256,512]{1,0:T(8,128)(2,1)S(1)}, bf16[256,512]{1,0:T(8,128)(2,1)S(1)}, u32[]{:S(2)}, u32[]{:S(2)}) collective-permute-start(bf16[256,512]{1,0:T(8,128)(2,1)S(1)} %shard_map.129.refs_0_.refs_2_.refs_1_), channel_id=1, source_target_pairs={{0,1},{1,4},{4,5},{5,8},{8,9},{9,12},{12,13},{13,0},{2,3},{3,6},{6... | collective-permute-start | bytes 786440 | tf_op jit(solution)/shard_map/ppermute | solution.py:23
  124.4 4.4 %collective-permute-done.19.refs_5_ = bf16[256,512]{1,0:T(8,128)(2,1)S(1)} collective-permute-done((bf16[256,512]{1,0:T(8,128)(2,1)S(1)}, bf16[256,512]{1,0:T(8,128)(2,1)S(1)}, u32[]{:S(2)}, u32[]{:S(2)}) %collective-permute-start.19) | collective-permute-done | bytes 262176 | tf_op jit(solution)/shard_map/ppermute | solution.py:23
  129.9 6.1 %attend.8 = (bf16[256,1280]{1,0:T(8,128)(2,1)S(1)}, bf16[256,512]{1,0:T(8,128)(2,1)S(1)}) custom-call(f32[14]{0:T(128)S(1)} %select_n.43.refs_10_.bias, bf16[256,1792]{1,0:T(8,128)(2,1)S(1)} %shard_map.128.refs_0_.query, bf16[256,512]{1,0:T(8,128)(2,1)S(1)} %shard_map.127.refs_0_.refs_1_, bf16[256,512]{1,0:T(8,128)(2,1)S(1)} %shard_map.131.refs_1_.refs_6_.refs_0_.refs_2_, ...), custom_call_target="tpu_custom_call" | custom-call | flops 1644167168 | tf_op jit(solution)/shard_map/attend/pallas_call | solution.py:174
  136.0 5.0 %shard_map.132.refs_0_.query = bf16[256,1792]{1,0:T(8,128)(2,1)S(1)} custom-call(bf16[1024,1792]{1,0:T(8,128)(2,1)S(1)} %copy-done.2, bf16[256,1792]{1,0:T(8,128)(2,1)S(1)} %collective-permute-done.4.tb.refs_0_, bf16[1792,1792]{1,0:T(8,128)(2,1)S(1)} %get-tuple-element.23.refs_0_.wa, bf16[1792,1792]{1,0:T(8,128)(2,1)S(1)} %get-tuple-element.24.wb, ...), custom_call_target="tpu_custom_call" | custom-call | flops 3288334336 | tf_op jit(solution)/shard_map/pallas_call | solution.py:117
  152.2 6.1 %attend.9 = (bf16[256,1280]{1,0:T(8,128)(2,1)S(1)}, bf16[256,512]{1,0:T(8,128)(2,1)S(1)}) custom-call(f32[14]{0:T(128)S(1)} %select_n.45.refs_11_.bias, bf16[256,1792]{1,0:T(8,128)(2,1)S(1)} %shard_map.130.refs_8_.query, bf16[256,512]{1,0:T(8,128)(2,1)S(1)} %shard_map.129.refs_0_.refs_2_.refs_1_, ...), custom_call_target="tpu_custom_call" | custom-call | flops 1644167168 | tf_op jit(solution)/shard_map/attend/pallas_call | solution.py:174
  159.2 5.6 %collective-permute-done.23.refs_5_ = bf16[256,512]{1,0:T(8,128)(2,1)S(1)} collective-permute-done((bf16[256,512]{1,0:T(8,128)(2,1)S(1)}, bf16[256,512]{1,0:T(8,128)(2,1)S(1)}, u32[]{:S(2)}, u32[]{:S(2)}) %collective-permute-start.23) | collective-permute-done | bytes 262176 | tf_op jit(solution)/shard_map/ppermute | solution.py:23
  164.8 6.1 %attend.10 = (bf16[256,1280]{1,0:T(8,128)(2,1)S(1)}, bf16[256,512]{1,0:T(8,128)(2,1)S(1)}) custom-call(f32[14]{0:T(128)S(1)} %select_n.47.refs_12_.bias, bf16[256,1792]{1,0:T(8,128)(2,1)S(1)} %shard_map.132.refs_0_.query, bf16[256,512]{1,0:T(8,128)(2,1)S(1)} %shard_map.131.refs_1_.refs_6_.refs_0_.refs_2_, ...), custom_call_target="tpu_custom_call" | custom-call | flops 1644167168 | tf_op jit(solution)/shard_map/attend/pallas_call | solution.py:174
  170.9 5.0 %shard_map.134.query.refs_6_ = bf16[256,1792]{1,0:T(8,128)(2,1)S(1)} custom-call(bf16[1024,1792]{1,0:T(8,128)(2,1)S(1)} %copy-done.2, bf16[256,1792]{1,0:T(8,128)(2,1)S(1)} %collective-permute-done.tb.refs_1_, bf16[1792,1792]{1,0:T(8,128)(2,1)S(1)} %get-tuple-element.23.refs_0_.wa, bf16[1792,1792]{1,0:T(8,128)(2,1)S(1)} %get-tuple-element.24.wb, ...), custom_call_target="tpu_custom_call" | custom-call | flops 3288334336 | tf_op jit(solution)/shard_map/pallas_call | solution.py:117
  175.9 8.9 %collective-permute-done.28.refs_5_ = bf16[256,512]{1,0:T(8,128)(2,1)S(1)} collective-permute-done((bf16[256,512]{1,0:T(8,128)(2,1)S(1)}, bf16[256,512]{1,0:T(8,128)(2,1)S(1)}, u32[]{:S(2)}, u32[]{:S(2)}) %collective-permute-start.28) | collective-permute-done | bytes 262176 | tf_op jit(solution)/shard_map/ppermute | solution.py:23
  185.6 6.2 %attend.11 = (bf16[256,1280]{1,0:T(8,128)(2,1)S(1)}, bf16[256,512]{1,0:T(8,128)(2,1)S(1)}) custom-call(f32[14]{0:T(128)S(1)} %select_n.41.refs_13_.bias, bf16[256,1792]{1,0:T(8,128)(2,1)S(1)} %shard_map.134.query.refs_6_, bf16[256,512]{1,0:T(8,128)(2,1)S(1)} %shard_map.133.refs_7_.refs_0_, bf16[256,512]{1,0:T(8,128)(2,1)S(1)} %shard_map.127.refs_0_.refs_1_, ...), custom_call_target="tpu_custom_call" | custom-call | flops 1644167168 | tf_op jit(solution)/shard_map/attend/pallas_call | solution.py:174
  194.0 7.4 %collective-permute-done.35.refs_4_ = bf16[512,256]{1,0:T(8,128)(2,1)S(1)} collective-permute-done((bf16[512,256]{1,0:T(8,128)(2,1)S(1)}, bf16[512,256]{1,0:T(8,128)(2,1)S(1)}, u32[]{:S(2)}, u32[]{:S(2)}) %collective-permute-start.35) | collective-permute-done | bytes 262176 | tf_op jit(solution)/shard_map/ppermute | solution.py:23
  215.6 14.0 %collective-permute-done.38.refs_4_ = bf16[256,1280]{1,0:T(8,128)(2,1)S(1)} collective-permute-done((bf16[256,1280]{1,0:T(8,128)(2,1)S(1)}, bf16[256,1280]{1,0:T(8,128)(2,1)S(1)}, u32[]{:S(2)}, u32[]{:S(2)}) %collective-permute-start.38) | collective-permute-done | bytes 655392 | tf_op jit(solution)/shard_map/ppermute | solution.py:27
  231.7 5.1 %collective-permute-done.29.refs_0_ = bf16[256,1280]{1,0:T(8,128)(2,1)S(1)} collective-permute-done((bf16[256,1280]{1,0:T(8,128)(2,1)S(1)}, bf16[256,1280]{1,0:T(8,128)(2,1)S(1)}, u32[]{:S(2)}, u32[]{:S(2)}) %collective-permute-start.29) | collective-permute-done | bytes 655392 | tf_op jit(solution)/shard_map/ppermute | solution.py:27
  (127 shorter events, 69.4 us)
Async XLA Ops:
  0.0 38.6 %collective-permute-start.1 = (bf16[1792,1792]{1,0:T(8,128)(2,1)}, bf16[1792,1792]{1,0:T(8,128)(2,1)}, u32[]{:S(2)}, u32[]{:S(2)}) collective-permute-start(bf16[1792,1792]{1,0:T(8,128)(2,1)} %wq.1), channel_id=1, source_target_pairs={{0,1},{1,0},{2,3},{3,2},{4,5},{5,4},{6,7},{7,6},{8,9},{9,8},{10,11... | collective-permute-start | bytes 19267592 | tf_op jit(solution)/shard_map/ppermute | solution.py:27
  6.7 22.2 %collective-permute-start.2 = (bf16[1792,256]{1,0:T(8,128)(2,1)}, bf16[1792,256]{1,0:T(8,128)(2,1)S(1)}, u32[]{:S(2)}, u32[]{:S(2)}) collective-permute-start(bf16[1792,256]{1,0:T(8,128)(2,1)} %wk.1), channel_id=1, source_target_pairs={{0,1},{1,0},{2,3},{3,2},{4,5},{5,4},{6,7},{7,6},{8,9},{9,8},{10,11... | collective-permute-start | bytes 2752520 | tf_op jit(solution)/shard_map/ppermute | solution.py:27
  7.0 30.8 %collective-permute-start.3 = (bf16[1792,256]{1,0:T(8,128)(2,1)}, bf16[1792,256]{1,0:T(8,128)(2,1)}, u32[]{:S(2)}, u32[]{:S(2)}) collective-permute-start(bf16[1792,256]{1,0:T(8,128)(2,1)} %wv.1), channel_id=1, source_target_pairs={{0,1},{1,0},{2,3},{3,2},{4,5},{5,4},{6,7},{7,6},{8,9},{9,8},{10,11... | collective-permute-start | bytes 2752520 | tf_op jit(solution)/shard_map/ppermute | solution.py:27
  8.4 38.8 %collective-permute-start.5 = (bf16[256,1792]{1,0:T(8,128)(2,1)}, bf16[256,1792]{1,0:T(8,128)(2,1)S(1)}, u32[]{:S(2)}, u32[]{:S(2)}) collective-permute-start(bf16[256,1792]{1,0:T(8,128)(2,1)} %cut.6), channel_id=1, source_target_pairs={{0,2},{2,0},{1,3},{3,1},{4,6},{6,4},{5,7},{7,5},{8,10},{10,8},{9,1... | collective-permute-start | bytes 2752520 | tf_op jit(solution)/shard_map/ppermute | solution.py:27
  29.8 25.2 %collective-permute-start.6 = (bf16[256,1792]{1,0:T(8,128)(2,1)}, bf16[256,1792]{1,0:T(8,128)(2,1)S(1)}, u32[]{:S(2)}, u32[]{:S(2)}) collective-permute-start(bf16[256,1792]{1,0:T(8,128)(2,1)} %cut.7), channel_id=1, source_target_pairs={{0,2},{2,0},{1,3},{3,1},{4,6},{6,4},{5,7},{7,5},{8,10},{10,8},{9,1... | collective-permute-start | bytes 2752520 | tf_op jit(solution)/shard_map/ppermute | solution.py:27
  37.8 23.4 %collective-permute-start.11 = (bf16[224,768]{1,0:T(8,128)(2,1)S(1)}, bf16[224,768]{1,0:T(8,128)(2,1)S(1)}, u32[]{:S(2)}, u32[]{:S(2)}) collective-permute-start(bf16[224,768]{1,0:T(8,128)(2,1)S(1)} %collective-permute-done.7.refs_0_), channel_id=1, source_target_pairs={{0,16},{16,0},{1,17},{17,1},{2,18},{18,2},{3,19},{19,3},{4,20},{20... | collective-permute-start | bytes 1032200 | tf_op jit(solution)/shard_map/ppermute | solution.py:27
  38.6 22.6 %collective-permute-start.12 = (bf16[224,768]{1,0:T(8,128)(2,1)}, bf16[224,768]{1,0:T(8,128)(2,1)S(1)}, u32[]{:S(2)}, u32[]{:S(2)}) collective-permute-start(bf16[224,768]{1,0:T(8,128)(2,1)} %collective-permute-done.8.refs_1_), channel_id=1, source_target_pairs={{0,16},{16,0},{1,17},{17,1},{2,18},{18,2},{3,19},{19,3},{4,20},{20... | collective-permute-start | bytes 1032200 | tf_op jit(solution)/shard_map/ppermute | solution.py:27
  72.7 44.9 %collective-permute-start.4 = (bf16[256,1792]{1,0:T(8,128)(2,1)S(1)}, bf16[256,1792]{1,0:T(8,128)(2,1)S(1)}, u32[]{:S(2)}, u32[]{:S(2)}) collective-permute-start(bf16[256,1792]{1,0:T(8,128)(2,1)S(1)} %cut.5), channel_id=1, source_target_pairs={{0,2},{2,0},{1,3},{3,1},{4,6},{6,4},{5,7},{7,5},{8,10},{10,8},{9,1... | collective-permute-start | bytes 2752520 | tf_op jit(solution)/shard_map/ppermute | solution.py:27
  73.5 40.8 %collective-permute-start.18 = (bf16[256,512]{1,0:T(8,128)(2,1)S(1)}, bf16[256,512]{1,0:T(8,128)(2,1)S(1)}, u32[]{:S(2)}, u32[]{:S(2)}) collective-permute-start(bf16[256,512]{1,0:T(8,128)(2,1)S(1)} %shard_map.127.refs_0_.refs_1_), channel_id=1, source_target_pairs={{0,4},{4,8},{8,12},{12,0},{1,5},{5,9},{9,13},{13,1},{2,6},{6,10},{... | collective-permute-start | bytes 786440 | tf_op jit(solution)/shard_map/ppermute | solution.py:23
  73.8 67.3 %collective-permute-start = (bf16[256,1792]{1,0:T(8,128)(2,1)S(1)}, bf16[256,1792]{1,0:T(8,128)(2,1)S(1)}, u32[]{:S(2)}, u32[]{:S(2)}) collective-permute-start(bf16[256,1792]{1,0:T(8,128)(2,1)S(1)} %cut.4), channel_id=1, source_target_pairs={{0,2},{2,0},{1,3},{3,1},{4,6},{6,4},{5,7},{7,5},{8,10},{10,8},{9,1... | collective-permute-start | bytes 2752520 | tf_op jit(solution)/shard_map/ppermute | solution.py:27
  74.6 39.8 %collective-permute-start.16 = (f32[1,768]{1,0:T(1,128)S(1)}, f32[1,768]{1,0:T(1,128)S(1)}, u32[]{:S(2)}, u32[]{:S(2)}) collective-permute-start(f32[1,768]{1,0:T(1,128)S(1)} %broadcast_in_dim.42), channel_id=1, source_target_pairs={{0,2},{2,0},{1,3},{3,1},{4,6},{6,4},{5,7},{7,5},{8,10},{10,8},{9,1... | collective-permute-start | bytes 9224 | tf_op jit(solution)/shard_map/ppermute | solution.py:27
  77.2 47.2 %collective-permute-start.17 = (bf16[256,512]{1,0:T(8,128)(2,1)S(1)}, bf16[256,512]{1,0:T(8,128)(2,1)S(1)}, u32[]{:S(2)}, u32[]{:S(2)}) collective-permute-start(bf16[256,512]{1,0:T(8,128)(2,1)S(1)} %shard_map.127.refs_0_.refs_1_), channel_id=1, source_target_pairs={{0,1},{1,4},{4,5},{5,8},{8,9},{9,12},{12,13},{13,0},{2,3},{3,6},{6... | collective-permute-start | bytes 786440 | tf_op jit(solution)/shard_map/ppermute | solution.py:23
  117.5 24.8 %collective-permute-start.24 = (bf16[256,512]{1,0:T(8,128)(2,1)S(1)}, bf16[256,512]{1,0:T(8,128)(2,1)S(1)}, u32[]{:S(2)}, u32[]{:S(2)}) collective-permute-start(bf16[256,512]{1,0:T(8,128)(2,1)S(1)} %shard_map.129.refs_0_.refs_2_.refs_1_), channel_id=1, source_target_pairs={{0,1},{1,4},{4,5},{5,8},{8,9},{9,12},{12,13},{13,0},{2,3},{3,6},{6... | collective-permute-start | bytes 786440 | tf_op jit(solution)/shard_map/ppermute | solution.py:23
  123.2 26.2 %collective-permute-start.26 = (bf16[256,512]{1,0:T(8,128)(2,1)S(1)}, bf16[256,512]{1,0:T(8,128)(2,1)S(1)}, u32[]{:S(2)}, u32[]{:S(2)}) collective-permute-start(bf16[256,512]{1,0:T(8,128)(2,1)S(1)} %collective-permute-done.25.refs_4_), channel_id=1, source_target_pairs={{0,4},{4,8},{8,12},{12,0},{1,5},{5,9},{9,13},{13,1},{2,6},{6,10},{... | collective-permute-start | bytes 786440 | tf_op jit(solution)/shard_map/ppermute | solution.py:23
  128.8 29.5 %collective-permute-start.21 = (bf16[256,512]{1,0:T(8,128)(2,1)S(1)}, bf16[256,512]{1,0:T(8,128)(2,1)S(1)}, u32[]{:S(2)}, u32[]{:S(2)}) collective-permute-start(bf16[256,512]{1,0:T(8,128)(2,1)S(1)} %shard_map.131.refs_1_.refs_6_.refs_0_.refs_2_), channel_id=1, source_target_pairs={{0,1},{1,4},{4,5},{5,8},{8,9},{9,12},{12,13},{13,0},{2,3},{3,6},{6... | collective-permute-start | bytes 786440 | tf_op jit(solution)/shard_map/ppermute | solution.py:23
  144.2 20.6 %collective-permute-start.23 = (bf16[256,512]{1,0:T(8,128)(2,1)S(1)}, bf16[256,512]{1,0:T(8,128)(2,1)S(1)}, u32[]{:S(2)}, u32[]{:S(2)}) collective-permute-start(bf16[256,512]{1,0:T(8,128)(2,1)S(1)} %collective-permute-done.22.refs_4_), channel_id=1, source_target_pairs={{0,4},{4,8},{8,12},{12,0},{1,5},{5,9},{9,13},{13,1},{2,6},{6,10},{... | collective-permute-start | bytes 786440 | tf_op jit(solution)/shard_map/ppermute | solution.py:23
  149.4 42.4 %collective-permute-start.34 = (bf16[512,256]{1,0:T(8,128)(2,1)S(1)}, bf16[512,256]{1,0:T(8,128)(2,1)S(1)}, u32[]{:S(2)}, u32[]{:S(2)}) collective-permute-start(bf16[512,256]{1,0:T(8,128)(2,1)S(1)} %get-tuple-element.29.refs_0_.refs_1_), channel_id=1, source_target_pairs={{0,4},{4,8},{8,12},{12,0},{1,5},{5,9},{9,13},{13,1},{2,6},{6,10},{... | collective-permute-start | bytes 786440 | tf_op jit(solution)/shard_map/ppermute | solution.py:23
  151.2 41.3 %collective-permute-start.33 = (bf16[512,256]{1,0:T(8,128)(2,1)S(1)}, bf16[512,256]{1,0:T(8,128)(2,1)S(1)}, u32[]{:S(2)}, u32[]{:S(2)}) collective-permute-start(bf16[512,256]{1,0:T(8,128)(2,1)S(1)} %get-tuple-element.29.refs_0_.refs_1_), channel_id=1, source_target_pairs={{0,1},{1,4},{4,5},{5,8},{8,9},{9,12},{12,13},{13,0},{2,3},{3,6},{6... | collective-permute-start | bytes 786440 | tf_op jit(solution)/shard_map/ppermute | solution.py:23
  158.3 35.0 %collective-permute-start.30 = (bf16[512,256]{1,0:T(8,128)(2,1)S(1)}, bf16[512,256]{1,0:T(8,128)(2,1)S(1)}, u32[]{:S(2)}, u32[]{:S(2)}) collective-permute-start(bf16[512,256]{1,0:T(8,128)(2,1)S(1)} %get-tuple-element.31.refs_6_.refs_1_.refs_0_), channel_id=1, source_target_pairs={{0,1},{1,4},{4,5},{5,8},{8,9},{9,12},{12,13},{13,0},{2,3},{3,6},{6... | collective-permute-start | bytes 786440 | tf_op jit(solution)/shard_map/ppermute | solution.py:23
  159.2 34.9 %collective-permute-start.31 = (bf16[512,256]{1,0:T(8,128)(2,1)S(1)}, bf16[512,256]{1,0:T(8,128)(2,1)S(1)}, u32[]{:S(2)}, u32[]{:S(2)}) collective-permute-start(bf16[512,256]{1,0:T(8,128)(2,1)S(1)} %get-tuple-element.31.refs_6_.refs_1_.refs_0_), channel_id=1, source_target_pairs={{0,4},{4,8},{8,12},{12,0},{1,5},{5,9},{9,13},{13,1},{2,6},{6,10},{... | collective-permute-start | bytes 786440 | tf_op jit(solution)/shard_map/ppermute | solution.py:23
  184.8 28.5 %collective-permute-start.36 = (bf16[256,1280]{1,0:T(8,128)(2,1)S(1)}, bf16[256,1280]{1,0:T(8,128)(2,1)S(1)}, u32[]{:S(2)}, u32[]{:S(2)}) collective-permute-start(bf16[256,1280]{1,0:T(8,128)(2,1)S(1)} %get-tuple-element.38.refs_0_), channel_id=1, source_target_pairs={{0,2},{2,0},{1,3},{3,1},{4,6},{6,4},{5,7},{7,5},{8,10},{10,8},{9,1... | collective-permute-start | bytes 1966088 | tf_op jit(solution)/shard_map/ppermute | solution.py:27
  191.8 23.8 %collective-permute-start.37 = (bf16[256,1280]{1,0:T(8,128)(2,1)S(1)}, bf16[256,1280]{1,0:T(8,128)(2,1)S(1)}, u32[]{:S(2)}, u32[]{:S(2)}) collective-permute-start(bf16[256,1280]{1,0:T(8,128)(2,1)S(1)} %get-tuple-element.39.refs_1_), channel_id=1, source_target_pairs={{0,2},{2,0},{1,3},{3,1},{4,6},{6,4},{5,7},{7,5},{8,10},{10,8},{9,1... | collective-permute-start | bytes 1966088 | tf_op jit(solution)/shard_map/ppermute | solution.py:27
  192.6 37.1 %collective-permute-start.38 = (bf16[256,1280]{1,0:T(8,128)(2,1)S(1)}, bf16[256,1280]{1,0:T(8,128)(2,1)S(1)}, u32[]{:S(2)}, u32[]{:S(2)}) collective-permute-start(bf16[256,1280]{1,0:T(8,128)(2,1)S(1)} %get-tuple-element.40.refs_2_), channel_id=1, source_target_pairs={{0,2},{2,0},{1,3},{3,1},{4,6},{6,4},{5,7},{7,5},{8,10},{10,8},{9,1... | collective-permute-start | bytes 1966088 | tf_op jit(solution)/shard_map/ppermute | solution.py:27
  193.3 43.5 %collective-permute-start.29 = (bf16[256,1280]{1,0:T(8,128)(2,1)S(1)}, bf16[256,1280]{1,0:T(8,128)(2,1)S(1)}, u32[]{:S(2)}, u32[]{:S(2)}) collective-permute-start(bf16[256,1280]{1,0:T(8,128)(2,1)S(1)} %get-tuple-element.34.refs_3_), channel_id=1, source_target_pairs={{0,2},{2,0},{1,3},{3,1},{4,6},{6,4},{5,7},{7,5},{8,10},{10,8},{9,1... | collective-permute-start | bytes 1966088 | tf_op jit(solution)/shard_map/ppermute | solution.py:27
  (27 other events, 373.5 us)

commit v3 on v2

--- a/solution.py
+++ b/solution.py
@@ -87,8 +87,10 @@
     )(flag, *own, *other, *deps)
 
 
-def project_body(row, tile, rot, ta, tb, wa, wb, bias, cos, sin, *refs):
-    out = refs[-1]
+def project_body(row, tile, rot, keep, ta, tb, wa, wb, bias, cos, sin, *refs):
+    out = refs[-2] if keep else refs[-1]
+    if keep:
+        refs[-1][...] = tb[...]
     rows = tb.shape[0]
     mine = pl.ds(row, rows)
 
@@ -111,14 +113,15 @@
         pl.loop(0, out.shape[1] // tile)(columns)
 
 
-def project(tokens, row, piece, wa, wb, bias, cos, sin, tile, rot, deps):
+def project(tokens, row, piece, wa, wb, bias, cos, sin, tile, rot, deps, keep=False):
     rows, half = piece.shape
     cols = wa.shape[1]
-    return pl.pallas_call(
-        functools.partial(project_body, row, tile, rot),
-        out_shape=jax.ShapeDtypeStruct((rows, cols), jnp.bfloat16),
+    out = jax.ShapeDtypeStruct((rows, cols), jnp.bfloat16)
+    return pl.pallas_call(
+        functools.partial(project_body, row, tile, rot, keep),
+        out_shape=(out, pltpu.VMEM(piece.shape, piece.dtype)) if keep else out,
         in_specs=[VMEM] * 7 + [ANY] * len(deps),
-        out_specs=VMEM,
+        out_specs=(VMEM, VMEM) if keep else VMEM,
         compiler_params=params(5),
         cost_estimate=pl.CostEstimate(flops=4 * rows * half * cols, bytes_accessed=0, transcendentals=0),
     )(tokens, piece, wa, wb, bias, cos, sin, *deps)
@@ -471,7 +474,12 @@
 
     def keys_values(i, deps):
         (b, n), piece = runs[i], pieces[i]
-        kv = project(tokens, b * BLOCK, piece, wkva, wkvb, kvb, cos, sin, 2 * kvl * HD, kvl, deps)
+        kv = project(
+            tokens, b * BLOCK, piece, wkva, wkvb, kvb, cos, sin, 2 * kvl * HD, kvl, deps,
+            paired and i % 2 == 0,
+        )
+        if paired and i % 2 == 0:
+            kv, pieces[i] = kv
         exchanged(kv, range(b, b + n), sources)
         return (kv,)
 

time: 239 us -> 239 us (level)
  no operation moved by 1% of the time
where the time goes in v3:
time: 239 us; the launch traced here: 238 us
  waiting for transfers between devices  110 us (46%)
  Pallas kernels  81.2 us (34%)
  starting transfers between devices  31.1 us (13%)
  local copies, waits for them, and re-layouts  10.3 us (4%)
  other arithmetic  5.18 us (2%)
    ppermute x18, waiting for transfers between devices, swapped(): return lax.ppermute(value, axis, [(0, 1), (1, 0)])  71.8 us
    ppermute x21, waiting for transfers between devices, shifted(): lax.ppermute(value, axis, [(s, (s + steps) % count) for s in range(count)])  38.1 us
    pallas_call x8, Pallas kernels, attend(): pl.pallas_call(functools.partial(attend_body, plan, len(arrays), q_row, g...  33.7 us
    pallas_call x8, Pallas kernels, project(): pl.pallas_call(functools.partial(project_body, row, tile, rot, keep), out...  24.9 us
    ppermute x18, starting transfers between devices, swapped(): return lax.ppermute(value, axis, [(0, 1), (1, 0)])  16.6 us
    ppermute x21, starting transfers between devices, shifted(): lax.ppermute(value, axis, [(s, (s + steps) % count) for s in range(count)])  14.5 us
    unnamed x24, local copies, waits for them, and re-layouts  9.97 us
    pallas_call x2, Pallas kernels, project_shared(): pl.pallas_call(functools.partial(project_shared_body, bases), out_shape=(...  6.3 us
  transfers between devices with their start and end apart: 39, of which 15 were waited for; matrix products, arithmetic and copies ran while one was open for 2% of the time, Pallas kernels for 33%

profile of v3, /device:TPU:1, one launch (start us, length us, event | category | flops | bytes accessed | tf_op | source)
XLA Modules:
  0.0 238.4 jit_solution(14581304037892909712)
XLA Ops:
  8.6 6.5 %collective-permute-done.7.refs_0_ = bf16[224,768]{1,0:T(8,128)(2,1)S(1)} collective-permute-done((bf16[224,768]{1,0:T(8,128)(2,1)S(1)}, bf16[224,768]{1,0:T(8,128)(2,1)S(1)}, u32[]{:S(2)}, u32[]{:S(2)}) %collective-permute-start.7) | collective-permute-done | bytes 344096 | tf_op jit(solution)/shard_map/ppermute | solution.py:27
  16.4 3.2 %fusion = (f32[1024,64]{1,0:T(8,128)}, f32[1024,64]{1,0:T(8,128)}, f32[1024,64]{1,0:T(8,128)}) fusion(f32[64]{0:T(128)S(1)} %multiply_exponential_fusion, f32[1024]{0:T(1024)S(1)} %add_convert_fusion), kind=kLoop, calls=%fused_computation.4 | loop fusion | flops 131072 | bytes 790784 | tf_op jit(solution)/shard_map/neg | solution.py:36
  19.6 6.0 %collective-permute-done.8.refs_1_ = bf16[224,768]{1,0:T(8,128)(2,1)} collective-permute-done((bf16[224,768]{1,0:T(8,128)(2,1)S(1)}, bf16[224,768]{1,0:T(8,128)(2,1)}, u32[]{:S(2)}, u32[]{:S(2)}) %collective-permute-start.8) | collective-permute-done | bytes 344096 | tf_op jit(solution)/shard_map/ppermute | solution.py:23
  30.9 4.6 %collective-permute-done.9.refs_2_ = bf16[224,768]{1,0:T(8,128)(2,1)} collective-permute-done((bf16[224,768]{1,0:T(8,128)(2,1)}, bf16[224,768]{1,0:T(8,128)(2,1)}, u32[]{:S(2)}, u32[]{:S(2)}) %collective-permute-start.9) | collective-permute-done | bytes 344096 | tf_op jit(solution)/shard_map/ppermute | solution.py:23
  43.3 3.9 %stage.1 = (bf16[1792,1792]{1,0:T(8,128)(2,1)S(1)}, bf16[1792,512]{1,0:T(8,128)(2,1)S(1)}, bf16[1792,1792]{1,0:T(8,128)(2,1)S(1)}, bf16[1792,512]{1,0:T(8,128)(2,1)S(1)}) custom-call(s32[1]{0:T(128)} %bitcast.flag.refs_0_, bf16[1792,1792]{1,0:T(8,128)(2,1)S(1)} %copy-done.4, bf16[1792,256]{1,0:T(8,128)(2,1)} %wk.1, bf16[1792,256]{1,0:T(8,128)(2,1)} %wv.1, ...), custom_call_target="tpu_custom_call" | custom-call | bytes 16515072 | tf_op jit(solution)/shard_map/stage/pallas_call | solution.py:78
  50.0 5.0 %shard_map.128.refs_0_.query = bf16[256,1792]{1,0:T(8,128)(2,1)S(1)} custom-call(bf16[1024,1792]{1,0:T(8,128)(2,1)S(1)} %copy-done.2, bf16[256,1792]{1,0:T(8,128)(2,1)S(1)} %get-tuple-element.31.tb.refs_0_, bf16[1792,1792]{1,0:T(8,128)(2,1)S(1)} %get-tuple-element.27.refs_0_.wa, bf16[1792,1792]{1,0:T(8,128)(2,1)S(1)} %get-tuple-element.28.wb, ...), custom_call_target="tpu_custom_call" | custom-call | flops 3288334336 | tf_op jit(solution)/shard_map/pallas_call | solution.py:120
  56.2 5.0 %shard_map.130.refs_8_.query = bf16[256,1792]{1,0:T(8,128)(2,1)S(1)} custom-call(bf16[1024,1792]{1,0:T(8,128)(2,1)S(1)} %copy-done.2, bf16[256,1792]{1,0:T(8,128)(2,1)S(1)} %collective-permute-done.6.tb.refs_1_, bf16[1792,1792]{1,0:T(8,128)(2,1)S(1)} %get-tuple-element.27.refs_0_.wa, bf16[1792,1792]{1,0:T(8,128)(2,1)S(1)} %get-tuple-element.28.wb, ...), custom_call_target="tpu_custom_call" | custom-call | flops 3288334336 | tf_op jit(solution)/shard_map/pallas_call | solution.py:120
  61.3 5.6 %collective-permute-done.14.refs_7_ = bf16[224,768]{1,0:T(8,128)(2,1)S(1)} collective-permute-done((bf16[224,768]{1,0:T(8,128)(2,1)}, bf16[224,768]{1,0:T(8,128)(2,1)S(1)}, u32[]{:S(2)}, u32[]{:S(2)}) %collective-permute-start.14) | collective-permute-done | bytes 344096 | tf_op jit(solution)/shard_map/ppermute | solution.py:27
  68.8 3.7 %collective-permute-start.15 = (bf16[1792,768]{1,0:T(8,128)(2,1)S(1)}, bf16[1792,768]{1,0:T(8,128)(2,1)S(1)}, u32[]{:S(2)}, u32[]{:S(2)}) collective-permute-start(bf16[1792,768]{1,0:T(8,128)(2,1)S(1)} %gather.1.refs_1_.refs_3_), channel_id=1, source_target_pairs={{0,1},{1,0},{2,3},{3,2},{4,5},{5,4},{6,7},{7,6},{8,9},{9,8},{10,11... | collective-permute-start | bytes 8257544 | tf_op jit(solution)/shard_map/ppermute | solution.py:27
  77.9 36.5 %collective-permute-done.16.refs_4_ = f32[1,768]{1,0:T(1,128)S(1)} collective-permute-done((f32[1,768]{1,0:T(1,128)S(1)}, f32[1,768]{1,0:T(1,128)S(1)}, u32[]{:S(2)}, u32[]{:S(2)}) %collective-permute-start.16) | collective-permute-done | bytes 3104 | tf_op jit(solution)/shard_map/ppermute | solution.py:27
  114.4 3.2 %project_shared.2 = (bf16[512,512]{1,0:T(8,128)(2,1)S(1)}, bf16[512,256]{1,0:T(8,128)(2,1)S(1)}) custom-call(bf16[1024,1792]{1,0:T(8,128)(2,1)S(1)} %copy-done.2, bf16[256,1792]{1,0:T(8,128)(2,1)S(1)} %get-tuple-element.31.tb.refs_0_, bf16[256,1792]{1,0:T(8,128)(2,1)S(1)} %collective-permute-done.6.tb.refs_1_, ...), custom_call_target="tpu_custom_call" | custom-call | flops 2818572288 | tf_op jit(solution)/shard_map/project_shared/pallas_call | solution.py:259
  117.5 5.2 %collective-permute-start.24 = (bf16[256,512]{1,0:T(8,128)(2,1)S(1)}, bf16[256,512]{1,0:T(8,128)(2,1)S(1)}, u32[]{:S(2)}, u32[]{:S(2)}) collective-permute-start(bf16[256,512]{1,0:T(8,128)(2,1)S(1)} %shard_map.129.refs_0_.refs_2_.refs_1_), channel_id=1, source_target_pairs={{0,1},{1,4},{4,5},{5,8},{8,9},{9,12},{12,13},{13,0},{2,3},{3,6},{6... | collective-permute-start | bytes 786440 | tf_op jit(solution)/shard_map/ppermute | solution.py:23
  124.4 4.3 %collective-permute-done.19.refs_5_ = bf16[256,512]{1,0:T(8,128)(2,1)S(1)} collective-permute-done((bf16[256,512]{1,0:T(8,128)(2,1)S(1)}, bf16[256,512]{1,0:T(8,128)(2,1)S(1)}, u32[]{:S(2)}, u32[]{:S(2)}) %collective-permute-start.19) | collective-permute-done | bytes 262176 | tf_op jit(solution)/shard_map/ppermute | solution.py:23
  130.0 6.1 %attend.8 = (bf16[256,1280]{1,0:T(8,128)(2,1)S(1)}, bf16[256,512]{1,0:T(8,128)(2,1)S(1)}) custom-call(f32[14]{0:T(128)S(1)} %select_n.43.refs_10_.bias, bf16[256,1792]{1,0:T(8,128)(2,1)S(1)} %shard_map.128.refs_0_.query, bf16[256,512]{1,0:T(8,128)(2,1)S(1)} %get-tuple-element.32.refs_0_.refs_1_, ...), custom_call_target="tpu_custom_call" | custom-call | flops 1644167168 | tf_op jit(solution)/shard_map/attend/pallas_call | solution.py:177
  136.0 5.0 %shard_map.132.refs_0_.query = bf16[256,1792]{1,0:T(8,128)(2,1)S(1)} custom-call(bf16[1024,1792]{1,0:T(8,128)(2,1)S(1)} %copy-done.2, bf16[256,1792]{1,0:T(8,128)(2,1)S(1)} %get-tuple-element.36.tb.refs_0_, bf16[1792,1792]{1,0:T(8,128)(2,1)S(1)} %get-tuple-element.27.refs_0_.wa, bf16[1792,1792]{1,0:T(8,128)(2,1)S(1)} %get-tuple-element.28.wb, ...), custom_call_target="tpu_custom_call" | custom-call | flops 3288334336 | tf_op jit(solution)/shard_map/pallas_call | solution.py:120
  152.2 6.2 %attend.9 = (bf16[256,1280]{1,0:T(8,128)(2,1)S(1)}, bf16[256,512]{1,0:T(8,128)(2,1)S(1)}) custom-call(f32[14]{0:T(128)S(1)} %select_n.45.refs_11_.bias, bf16[256,1792]{1,0:T(8,128)(2,1)S(1)} %shard_map.130.refs_8_.query, bf16[256,512]{1,0:T(8,128)(2,1)S(1)} %shard_map.129.refs_0_.refs_2_.refs_1_, ...), custom_call_target="tpu_custom_call" | custom-call | flops 1644167168 | tf_op jit(solution)/shard_map/attend/pallas_call | solution.py:177
  159.2 5.6 %collective-permute-done.23.refs_5_ = bf16[256,512]{1,0:T(8,128)(2,1)S(1)} collective-permute-done((bf16[256,512]{1,0:T(8,128)(2,1)S(1)}, bf16[256,512]{1,0:T(8,128)(2,1)S(1)}, u32[]{:S(2)}, u32[]{:S(2)}) %collective-permute-start.23) | collective-permute-done | bytes 262176 | tf_op jit(solution)/shard_map/ppermute | solution.py:23
  164.8 6.1 %attend.10 = (bf16[256,1280]{1,0:T(8,128)(2,1)S(1)}, bf16[256,512]{1,0:T(8,128)(2,1)S(1)}) custom-call(f32[14]{0:T(128)S(1)} %select_n.47.refs_12_.bias, bf16[256,1792]{1,0:T(8,128)(2,1)S(1)} %shard_map.132.refs_0_.query, bf16[256,512]{1,0:T(8,128)(2,1)S(1)} %get-tuple-element.37.refs_1_.refs_6_.refs_0_.refs_2_, ...), custom_call_target="tpu_custom_call" | custom-call | flops 1644167168 | tf_op jit(solution)/shard_map/attend/pallas_call | solution.py:177
  170.9 5.0 %shard_map.134.query.refs_6_ = bf16[256,1792]{1,0:T(8,128)(2,1)S(1)} custom-call(bf16[1024,1792]{1,0:T(8,128)(2,1)S(1)} %copy-done.2, bf16[256,1792]{1,0:T(8,128)(2,1)S(1)} %collective-permute-done.tb.refs_1_, bf16[1792,1792]{1,0:T(8,128)(2,1)S(1)} %get-tuple-element.27.refs_0_.wa, bf16[1792,1792]{1,0:T(8,128)(2,1)S(1)} %get-tuple-element.28.wb, ...), custom_call_target="tpu_custom_call" | custom-call | flops 3288334336 | tf_op jit(solution)/shard_map/pallas_call | solution.py:120
  175.9 8.9 %collective-permute-done.28.refs_5_ = bf16[256,512]{1,0:T(8,128)(2,1)S(1)} collective-permute-done((bf16[256,512]{1,0:T(8,128)(2,1)S(1)}, bf16[256,512]{1,0:T(8,128)(2,1)S(1)}, u32[]{:S(2)}, u32[]{:S(2)}) %collective-permute-start.28) | collective-permute-done | bytes 262176 | tf_op jit(solution)/shard_map/ppermute | solution.py:23
  185.6 6.2 %attend.11 = (bf16[256,1280]{1,0:T(8,128)(2,1)S(1)}, bf16[256,512]{1,0:T(8,128)(2,1)S(1)}) custom-call(f32[14]{0:T(128)S(1)} %select_n.41.refs_13_.bias, bf16[256,1792]{1,0:T(8,128)(2,1)S(1)} %shard_map.134.query.refs_6_, bf16[256,512]{1,0:T(8,128)(2,1)S(1)} %shard_map.133.refs_7_.refs_0_, bf16[256,512]{1,0:T(8,128)(2,1)S(1)} %get-tuple-element.32.refs_0_.refs_1_, ...), custom_call_target="tpu_custom_call" | custom-call | flops 1644167168 | tf_op jit(solution)/shard_map/attend/pallas_call | solution.py:177
  194.1 7.4 %collective-permute-done.35.refs_4_ = bf16[512,256]{1,0:T(8,128)(2,1)S(1)} collective-permute-done((bf16[512,256]{1,0:T(8,128)(2,1)S(1)}, bf16[512,256]{1,0:T(8,128)(2,1)S(1)}, u32[]{:S(2)}, u32[]{:S(2)}) %collective-permute-start.35) | collective-permute-done | bytes 262176 | tf_op jit(solution)/shard_map/ppermute | solution.py:23
  215.6 14.0 %collective-permute-done.38.refs_4_ = bf16[256,1280]{1,0:T(8,128)(2,1)S(1)} collective-permute-done((bf16[256,1280]{1,0:T(8,128)(2,1)S(1)}, bf16[256,1280]{1,0:T(8,128)(2,1)S(1)}, u32[]{:S(2)}, u32[]{:S(2)}) %collective-permute-start.38) | collective-permute-done | bytes 655392 | tf_op jit(solution)/shard_map/ppermute | solution.py:27
  231.7 5.1 %collective-permute-done.29.refs_0_ = bf16[256,1280]{1,0:T(8,128)(2,1)S(1)} collective-permute-done((bf16[256,1280]{1,0:T(8,128)(2,1)S(1)}, bf16[256,1280]{1,0:T(8,128)(2,1)S(1)}, u32[]{:S(2)}, u32[]{:S(2)}) %collective-permute-start.29) | collective-permute-done | bytes 655392 | tf_op jit(solution)/shard_map/ppermute | solution.py:27
  (127 shorter events, 69.3 us)
Async XLA Ops:
  0.0 38.6 %collective-permute-start.1 = (bf16[1792,1792]{1,0:T(8,128)(2,1)}, bf16[1792,1792]{1,0:T(8,128)(2,1)}, u32[]{:S(2)}, u32[]{:S(2)}) collective-permute-start(bf16[1792,1792]{1,0:T(8,128)(2,1)} %wq.1), channel_id=1, source_target_pairs={{0,1},{1,0},{2,3},{3,2},{4,5},{5,4},{6,7},{7,6},{8,9},{9,8},{10,11... | collective-permute-start | bytes 19267592 | tf_op jit(solution)/shard_map/ppermute | solution.py:27
  6.7 22.2 %collective-permute-start.2 = (bf16[1792,256]{1,0:T(8,128)(2,1)}, bf16[1792,256]{1,0:T(8,128)(2,1)S(1)}, u32[]{:S(2)}, u32[]{:S(2)}) collective-permute-start(bf16[1792,256]{1,0:T(8,128)(2,1)} %wk.1), channel_id=1, source_target_pairs={{0,1},{1,0},{2,3},{3,2},{4,5},{5,4},{6,7},{7,6},{8,9},{9,8},{10,11... | collective-permute-start | bytes 2752520 | tf_op jit(solution)/shard_map/ppermute | solution.py:27
  7.0 30.8 %collective-permute-start.3 = (bf16[1792,256]{1,0:T(8,128)(2,1)}, bf16[1792,256]{1,0:T(8,128)(2,1)}, u32[]{:S(2)}, u32[]{:S(2)}) collective-permute-start(bf16[1792,256]{1,0:T(8,128)(2,1)} %wv.1), channel_id=1, source_target_pairs={{0,1},{1,0},{2,3},{3,2},{4,5},{5,4},{6,7},{7,6},{8,9},{9,8},{10,11... | collective-permute-start | bytes 2752520 | tf_op jit(solution)/shard_map/ppermute | solution.py:27
  8.4 38.8 %collective-permute-start.5 = (bf16[256,1792]{1,0:T(8,128)(2,1)}, bf16[256,1792]{1,0:T(8,128)(2,1)S(1)}, u32[]{:S(2)}, u32[]{:S(2)}) collective-permute-start(bf16[256,1792]{1,0:T(8,128)(2,1)} %cut.6), channel_id=1, source_target_pairs={{0,2},{2,0},{1,3},{3,1},{4,6},{6,4},{5,7},{7,5},{8,10},{10,8},{9,1... | collective-permute-start | bytes 2752520 | tf_op jit(solution)/shard_map/ppermute | solution.py:27
  29.8 25.2 %collective-permute-start.6 = (bf16[256,1792]{1,0:T(8,128)(2,1)}, bf16[256,1792]{1,0:T(8,128)(2,1)S(1)}, u32[]{:S(2)}, u32[]{:S(2)}) collective-permute-start(bf16[256,1792]{1,0:T(8,128)(2,1)} %cut.7), channel_id=1, source_target_pairs={{0,2},{2,0},{1,3},{3,1},{4,6},{6,4},{5,7},{7,5},{8,10},{10,8},{9,1... | collective-permute-start | bytes 2752520 | tf_op jit(solution)/shard_map/ppermute | solution.py:27
  37.8 23.5 %collective-permute-start.11 = (bf16[224,768]{1,0:T(8,128)(2,1)S(1)}, bf16[224,768]{1,0:T(8,128)(2,1)S(1)}, u32[]{:S(2)}, u32[]{:S(2)}) collective-permute-start(bf16[224,768]{1,0:T(8,128)(2,1)S(1)} %collective-permute-done.7.refs_0_), channel_id=1, source_target_pairs={{0,16},{16,0},{1,17},{17,1},{2,18},{18,2},{3,19},{19,3},{4,20},{20... | collective-permute-start | bytes 1032200 | tf_op jit(solution)/shard_map/ppermute | solution.py:27
  38.6 22.6 %collective-permute-start.12 = (bf16[224,768]{1,0:T(8,128)(2,1)}, bf16[224,768]{1,0:T(8,128)(2,1)S(1)}, u32[]{:S(2)}, u32[]{:S(2)}) collective-permute-start(bf16[224,768]{1,0:T(8,128)(2,1)} %collective-permute-done.8.refs_1_), channel_id=1, source_target_pairs={{0,16},{16,0},{1,17},{17,1},{2,18},{18,2},{3,19},{19,3},{4,20},{20... | collective-permute-start | bytes 1032200 | tf_op jit(solution)/shard_map/ppermute | solution.py:27
  72.7 44.9 %collective-permute-start.4 = (bf16[256,1792]{1,0:T(8,128)(2,1)S(1)}, bf16[256,1792]{1,0:T(8,128)(2,1)S(1)}, u32[]{:S(2)}, u32[]{:S(2)}) collective-permute-start(bf16[256,1792]{1,0:T(8,128)(2,1)S(1)} %cut.5), channel_id=1, source_target_pairs={{0,2},{2,0},{1,3},{3,1},{4,6},{6,4},{5,7},{7,5},{8,10},{10,8},{9,1... | collective-permute-start | bytes 2752520 | tf_op jit(solution)/shard_map/ppermute | solution.py:27
  73.5 40.8 %collective-permute-start.18 = (bf16[256,512]{1,0:T(8,128)(2,1)S(1)}, bf16[256,512]{1,0:T(8,128)(2,1)S(1)}, u32[]{:S(2)}, u32[]{:S(2)}) collective-permute-start(bf16[256,512]{1,0:T(8,128)(2,1)S(1)} %get-tuple-element.32.refs_0_.refs_1_), channel_id=1, source_target_pairs={{0,4},{4,8},{8,12},{12,0},{1,5},{5,9},{9,13},{13,1},{2,6},{6,10},{... | collective-permute-start | bytes 786440 | tf_op jit(solution)/shard_map/ppermute | solution.py:23
  73.8 67.3 %collective-permute-start = (bf16[256,1792]{1,0:T(8,128)(2,1)S(1)}, bf16[256,1792]{1,0:T(8,128)(2,1)S(1)}, u32[]{:S(2)}, u32[]{:S(2)}) collective-permute-start(bf16[256,1792]{1,0:T(8,128)(2,1)S(1)} %cut.4), channel_id=1, source_target_pairs={{0,2},{2,0},{1,3},{3,1},{4,6},{6,4},{5,7},{7,5},{8,10},{10,8},{9,1... | collective-permute-start | bytes 2752520 | tf_op jit(solution)/shard_map/ppermute | solution.py:27
  74.6 39.8 %collective-permute-start.16 = (f32[1,768]{1,0:T(1,128)S(1)}, f32[1,768]{1,0:T(1,128)S(1)}, u32[]{:S(2)}, u32[]{:S(2)}) collective-permute-start(f32[1,768]{1,0:T(1,128)S(1)} %broadcast_in_dim.42), channel_id=1, source_target_pairs={{0,2},{2,0},{1,3},{3,1},{4,6},{6,4},{5,7},{7,5},{8,10},{10,8},{9,1... | collective-permute-start | bytes 9224 | tf_op jit(solution)/shard_map/ppermute | solution.py:27
  77.2 47.2 %collective-permute-start.17 = (bf16[256,512]{1,0:T(8,128)(2,1)S(1)}, bf16[256,512]{1,0:T(8,128)(2,1)S(1)}, u32[]{:S(2)}, u32[]{:S(2)}) collective-permute-start(bf16[256,512]{1,0:T(8,128)(2,1)S(1)} %get-tuple-element.32.refs_0_.refs_1_), channel_id=1, source_target_pairs={{0,1},{1,4},{4,5},{5,8},{8,9},{9,12},{12,13},{13,0},{2,3},{3,6},{6... | collective-permute-start | bytes 786440 | tf_op jit(solution)/shard_map/ppermute | solution.py:23
  117.5 24.8 %collective-permute-start.24 = (bf16[256,512]{1,0:T(8,128)(2,1)S(1)}, bf16[256,512]{1,0:T(8,128)(2,1)S(1)}, u32[]{:S(2)}, u32[]{:S(2)}) collective-permute-start(bf16[256,512]{1,0:T(8,128)(2,1)S(1)} %shard_map.129.refs_0_.refs_2_.refs_1_), channel_id=1, source_target_pairs={{0,1},{1,4},{4,5},{5,8},{8,9},{9,12},{12,13},{13,0},{2,3},{3,6},{6... | collective-permute-start | bytes 786440 | tf_op jit(solution)/shard_map/ppermute | solution.py:23
  123.2 26.2 %collective-permute-start.26 = (bf16[256,512]{1,0:T(8,128)(2,1)S(1)}, bf16[256,512]{1,0:T(8,128)(2,1)S(1)}, u32[]{:S(2)}, u32[]{:S(2)}) collective-permute-start(bf16[256,512]{1,0:T(8,128)(2,1)S(1)} %collective-permute-done.25.refs_4_), channel_id=1, source_target_pairs={{0,4},{4,8},{8,12},{12,0},{1,5},{5,9},{9,13},{13,1},{2,6},{6,10},{... | collective-permute-start | bytes 786440 | tf_op jit(solution)/shard_map/ppermute | solution.py:23
  128.8 29.6 %collective-permute-start.21 = (bf16[256,512]{1,0:T(8,128)(2,1)S(1)}, bf16[256,512]{1,0:T(8,128)(2,1)S(1)}, u32[]{:S(2)}, u32[]{:S(2)}) collective-permute-start(bf16[256,512]{1,0:T(8,128)(2,1)S(1)} %get-tuple-element.37.refs_1_.refs_6_.refs_0_.refs_2_), channel_id=1, source_target_pairs={{0,1},{1,4},{4,5},{5,8},{8,9},{9,12},{12,13},{13,0},{2,3},{3,6},{6... | collective-permute-start | bytes 786440 | tf_op jit(solution)/shard_map/ppermute | solution.py:23
  144.2 20.6 %collective-permute-start.23 = (bf16[256,512]{1,0:T(8,128)(2,1)S(1)}, bf16[256,512]{1,0:T(8,128)(2,1)S(1)}, u32[]{:S(2)}, u32[]{:S(2)}) collective-permute-start(bf16[256,512]{1,0:T(8,128)(2,1)S(1)} %collective-permute-done.22.refs_4_), channel_id=1, source_target_pairs={{0,4},{4,8},{8,12},{12,0},{1,5},{5,9},{9,13},{13,1},{2,6},{6,10},{... | collective-permute-start | bytes 786440 | tf_op jit(solution)/shard_map/ppermute | solution.py:23
  149.4 42.4 %collective-permute-start.34 = (bf16[512,256]{1,0:T(8,128)(2,1)S(1)}, bf16[512,256]{1,0:T(8,128)(2,1)S(1)}, u32[]{:S(2)}, u32[]{:S(2)}) collective-permute-start(bf16[512,256]{1,0:T(8,128)(2,1)S(1)} %get-tuple-element.35.refs_0_.refs_1_), channel_id=1, source_target_pairs={{0,4},{4,8},{8,12},{12,0},{1,5},{5,9},{9,13},{13,1},{2,6},{6,10},{... | collective-permute-start | bytes 786440 | tf_op jit(solution)/shard_map/ppermute | solution.py:23
  151.2 41.3 %collective-permute-start.33 = (bf16[512,256]{1,0:T(8,128)(2,1)S(1)}, bf16[512,256]{1,0:T(8,128)(2,1)S(1)}, u32[]{:S(2)}, u32[]{:S(2)}) collective-permute-start(bf16[512,256]{1,0:T(8,128)(2,1)S(1)} %get-tuple-element.35.refs_0_.refs_1_), channel_id=1, source_target_pairs={{0,1},{1,4},{4,5},{5,8},{8,9},{9,12},{12,13},{13,0},{2,3},{3,6},{6... | collective-permute-start | bytes 786440 | tf_op jit(solution)/shard_map/ppermute | solution.py:23
  158.4 35.0 %collective-permute-start.30 = (bf16[512,256]{1,0:T(8,128)(2,1)S(1)}, bf16[512,256]{1,0:T(8,128)(2,1)S(1)}, u32[]{:S(2)}, u32[]{:S(2)}) collective-permute-start(bf16[512,256]{1,0:T(8,128)(2,1)S(1)} %get-tuple-element.39.refs_6_.refs_1_.refs_0_), channel_id=1, source_target_pairs={{0,1},{1,4},{4,5},{5,8},{8,9},{9,12},{12,13},{13,0},{2,3},{3,6},{6... | collective-permute-start | bytes 786440 | tf_op jit(solution)/shard_map/ppermute | solution.py:23
  159.2 34.9 %collective-permute-start.31 = (bf16[512,256]{1,0:T(8,128)(2,1)S(1)}, bf16[512,256]{1,0:T(8,128)(2,1)S(1)}, u32[]{:S(2)}, u32[]{:S(2)}) collective-permute-start(bf16[512,256]{1,0:T(8,128)(2,1)S(1)} %get-tuple-element.39.refs_6_.refs_1_.refs_0_), channel_id=1, source_target_pairs={{0,4},{4,8},{8,12},{12,0},{1,5},{5,9},{9,13},{13,1},{2,6},{6,10},{... | collective-permute-start | bytes 786440 | tf_op jit(solution)/shard_map/ppermute | solution.py:23
  184.8 28.6 %collective-permute-start.36 = (bf16[256,1280]{1,0:T(8,128)(2,1)S(1)}, bf16[256,1280]{1,0:T(8,128)(2,1)S(1)}, u32[]{:S(2)}, u32[]{:S(2)}) collective-permute-start(bf16[256,1280]{1,0:T(8,128)(2,1)S(1)} %get-tuple-element.46.refs_0_), channel_id=1, source_target_pairs={{0,2},{2,0},{1,3},{3,1},{4,6},{6,4},{5,7},{7,5},{8,10},{10,8},{9,1... | collective-permute-start | bytes 1966088 | tf_op jit(solution)/shard_map/ppermute | solution.py:27
  191.8 23.8 %collective-permute-start.37 = (bf16[256,1280]{1,0:T(8,128)(2,1)S(1)}, bf16[256,1280]{1,0:T(8,128)(2,1)S(1)}, u32[]{:S(2)}, u32[]{:S(2)}) collective-permute-start(bf16[256,1280]{1,0:T(8,128)(2,1)S(1)} %get-tuple-element.47.refs_1_), channel_id=1, source_target_pairs={{0,2},{2,0},{1,3},{3,1},{4,6},{6,4},{5,7},{7,5},{8,10},{10,8},{9,1... | collective-permute-start | bytes 1966088 | tf_op jit(solution)/shard_map/ppermute | solution.py:27
  192.6 37.1 %collective-permute-start.38 = (bf16[256,1280]{1,0:T(8,128)(2,1)S(1)}, bf16[256,1280]{1,0:T(8,128)(2,1)S(1)}, u32[]{:S(2)}, u32[]{:S(2)}) collective-permute-start(bf16[256,1280]{1,0:T(8,128)(2,1)S(1)} %get-tuple-element.48.refs_2_), channel_id=1, source_target_pairs={{0,2},{2,0},{1,3},{3,1},{4,6},{6,4},{5,7},{7,5},{8,10},{10,8},{9,1... | collective-permute-start | bytes 1966088 | tf_op jit(solution)/shard_map/ppermute | solution.py:27
  193.4 43.5 %collective-permute-start.29 = (bf16[256,1280]{1,0:T(8,128)(2,1)S(1)}, bf16[256,1280]{1,0:T(8,128)(2,1)S(1)}, u32[]{:S(2)}, u32[]{:S(2)}) collective-permute-start(bf16[256,1280]{1,0:T(8,128)(2,1)S(1)} %get-tuple-element.42.refs_3_), channel_id=1, source_target_pairs={{0,2},{2,0},{1,3},{3,1},{4,6},{6,4},{5,7},{7,5},{8,10},{10,8},{9,1... | collective-permute-start | bytes 1966088 | tf_op jit(solution)/shard_map/ppermute | solution.py:27
  (27 other events, 373.5 us)
